TPU v7x, 256 devices: a whole 4x4x8 slice. The times are simulated.
256 devices in a mesh: pair: 64 (over y, z, x_hi), az: 2 (over x_lo), rg: 2 (over core).
Axes of the slice: x: 4 (x_hi: 2, x_lo: 2; x = x_hi * 2 + x_lo), y: 4, z: 8, core: 2. Of those that a mesh axis runs over, the one named last changes fastest.
Arguments:
- acquisitions: bfloat16 [1024, 2, 40, 5120], P('pair', None, 'az', 'rg'), may hold values from -8 to 8
- reference_index: int32 [256], P('pair'), may hold values from 0 to 1022, as said below
- secondary_index: int32 [256], P('pair'), may hold values from 1 to 1023, as said below
- pair_count: int32 [64], P('pair'), may hold values from 1 to 4, 160 in all
Outputs:
- interferogram: float32 [256, 2, 8, 256], P('pair', None, 'az', 'rg')
- coherence: float32 [256, 8, 256], P('pair', 'az', 'rg')
Inputs may be any that keep to these rules, and one draw needn't show every extreme that they name: `reference_index`: the slots of index d of pair name acquisitions from 16 * (d - 1) to 16 * (d + 2) - 1 only, clipped to the stack; on every index some slot names the lower end of that range. `secondary_index`: each slot's secondary acquisition lies 1 to 3 after its reference acquisition and within the same range as the reference indices of that index of pair.
All inputs are finite; a program needn't handle non-finite values. No bound on the sum of `pair_count` on one device may be relied on, other than what follows from the above.
Results may differ from a plain program's by a relative error of at most 0.0003.
Values may be sent and summed in bfloat16 or wider, within the bound.
A program may use at most 64 MiB of HBM per device.

v0:
```python
import jax
import jax.numpy as jnp
from jax import lax
from jax.sharding import PartitionSpec as P


def with_halo(array, sides, width):
    for axis, dim in sides:
        peers, length = (lax.axis_size(axis), array.shape[dim])
        up = [(i, (i + 1) % peers) for i in range(peers - 1)]
        down = [(j, i) for i, j in up]
        last = lax.slice_in_dim(array, length - width, length, axis=dim)
        leading = lax.slice_in_dim(array, 0, width, axis=dim)
        before = lax.ppermute(last, axis, up)
        after = lax.ppermute(leading, axis, down)
        array = jnp.concatenate([before, array, after], axis=dim)
    return array


def window_sum(products):
    line_count = products.shape[-2]
    sample_count = products.shape[-1]
    out_lines = (line_count - 6) // 5
    out_cols = (sample_count - 22) // 20
    out_row = lax.broadcasted_iota(jnp.int32, (out_lines, line_count), 0)
    line_pos = lax.broadcasted_iota(jnp.int32, (out_lines, line_count), 1)
    line_table = ((line_pos >= 5 * out_row) & (line_pos <= 5 * out_row + 10)).astype(jnp.float32)
    sample_pos = lax.broadcasted_iota(jnp.int32, (sample_count, out_cols), 0)
    out_col = lax.broadcasted_iota(jnp.int32, (sample_count, out_cols), 1)
    sample_table = ((sample_pos >= 20 * out_col + 1) & (sample_pos <= 20 * out_col + 41)).astype(
        jnp.float32
    )
    line_sums = jnp.einsum(
        "il,cls->cis",
        line_table,
        products,
        precision=lax.Precision.HIGHEST,
        preferred_element_type=jnp.float32,
    )
    return jnp.einsum(
        "cis,sj->cij",
        line_sums,
        sample_table,
        precision=lax.Precision.HIGHEST,
        preferred_element_type=jnp.float32,
    )


def pair_outputs(first_slab, second_slab):
    first_real = first_slab[0].astype(jnp.float32)
    first_imag = first_slab[1].astype(jnp.float32)
    second_real = second_slab[0].astype(jnp.float32)
    second_imag = second_slab[1].astype(jnp.float32)
    stacked = jnp.stack(
        [
            first_real * second_real + first_imag * second_imag,
            first_imag * second_real - first_real * second_imag,
            first_real * first_real + first_imag * first_imag,
            second_real * second_real + second_imag * second_imag,
        ]
    )
    window_sums = window_sum(stacked)
    interferogram = window_sums[0:2] / 451.0
    coherence = jnp.sqrt(
        window_sums[0] * window_sums[0] + window_sums[1] * window_sums[1]
    ) / jnp.sqrt(window_sums[2] * window_sums[3] + 1e-06)
    return (interferogram, coherence)


def on_device(acquisitions, reference_index, secondary_index, pair_count):
    block_rows = acquisitions.shape[0]
    slot_count = reference_index.shape[0]
    own_start = block_rows * lax.axis_index("pair")
    slots = jnp.arange(slot_count, dtype=jnp.int32)
    nearby = with_halo(acquisitions, (("pair", 0),), block_rows)
    block_start = own_start - block_rows

    def fetch_slab(name):
        return lax.dynamic_index_in_dim(nearby, name - block_start, 0, keepdims=False)

    def one_pair(items):
        first_slab = fetch_slab(items[1])
        second_slab = fetch_slab(items[2])
        stacked_pair = jnp.stack([first_slab, second_slab])
        stacked_pair = with_halo(stacked_pair, (("az", 2),), 3)
        stacked_pair = with_halo(stacked_pair, (("rg", 3),), 11)
        first_slab = stacked_pair[0]
        second_slab = stacked_pair[1]
        return pair_outputs(first_slab, second_slab)

    interferogram, coherence = lax.map(one_pair, (slots, reference_index, secondary_index))
    live_slots = slots < pair_count[0]
    interferogram = jnp.where(live_slots[:, None, None, None], interferogram, jnp.float32(0.0))
    coherence = jnp.where(live_slots[:, None, None], coherence, jnp.float32(0.0))
    return (interferogram, coherence)


def solution(mesh):
    return jax.shard_map(
        on_device,
        mesh=mesh,
        in_specs=(P("pair", None, "az", "rg"), P("pair"), P("pair"), P("pair")),
        out_specs=(P("pair", None, "az", "rg"), P("pair", "az", "rg")),
        check_vma=False,
    )
```

profile of v0, /device:TPU:1, one launch (start us, length us, event | category | flops | bytes accessed | tf_op | source)
XLA Modules:
  0.0 253.0 jit_solution(8768579190112217069)
XLA Ops:
  0.6 2.9 %copy.9 = bf16[16,2,20,2560]{3,0,2,1:T(8,128)(2,1)S(1)} copy(bf16[16,2,20,2560]{3,1,2,0:T(2,128)(2,1)} %param.6) | data formatting | bytes 6553600 | tf_op args[0]
  3.5 7.2 %collective-permute-start.4 = (bf16[16,2,20,2560]{3,0,2,1:T(8,128)(2,1)S(1)}, bf16[16,2,20,2560]{3,0,2,1:T(8,128)(2,1)}, u32[]{:S(2)}, u32[]{:S(2)}) collective-permute-start(bf16[16,2,20,2560]{3,0,2,1:T(8,128)(2,1)S(1)} %copy.9), channel_id=1, source_target_pairs={{0,4},{4,8},{8,12},{12,16},{16,20},{20,24},{24,28},{28,32},{32,36}... | collective-permute-start | bytes 9830408 | tf_op jit(solution)/shard_map/ppermute | solution.py:14
  12.7 136.1 %collective-permute-done.4 = bf16[16,2,20,2560]{3,0,2,1:T(8,128)(2,1)} collective-permute-done((bf16[16,2,20,2560]{3,0,2,1:T(8,128)(2,1)S(1)}, bf16[16,2,20,2560]{3,0,2,1:T(8,128)(2,1)}, u32[]{:S(2)}, u32[]{:S(2)}) %collective-permute-start.4) | collective-permute-done | bytes 3276832 | tf_op jit(solution)/shard_map/ppermute | solution.py:14
  148.8 7.2 %collective-permute-done.5 = bf16[16,2,20,2560]{3,0,2,1:T(8,128)(2,1)} collective-permute-done((bf16[16,2,20,2560]{3,0,2,1:T(8,128)(2,1)S(1)}, bf16[16,2,20,2560]{3,0,2,1:T(8,128)(2,1)}, u32[]{:S(2)}, u32[]{:S(2)}) %collective-permute-start.5) | collective-permute-done | bytes 3276832 | tf_op jit(solution)/shard_map/ppermute | solution.py:15
  156.0 4.5 %pad_maximum_fusion.3 = bf16[48,2,20,2560]{3,0,2,1:T(8,128)(2,1)S(1)} fusion(bf16[16,2,20,2560]{3,0,2,1:T(8,128)(2,1)} %collective-permute-done.5, bf16[16,2,20,2560]{3,0,2,1:T(8,128)(2,1)S(1)} %copy.9, bf16[16,2,20,2560]{3,0,2,1:T(8,128)(2,1)} %collective-permute-done.4), kind=kLoop, calls=%fused_computation.60 | loop fusion | flops 29491200 | bytes 19660800 | tf_op jit(solution)/shard_map/concatenate | solution.py:16
  160.5 16.2 %copy.12 = bf16[48,2,20,2560]{3,2,1,0:T(8,128)(2,1)} copy(bf16[48,2,20,2560]{3,0,2,1:T(8,128)(2,1)S(1)} %pad_maximum_fusion.3) | data formatting | bytes 19660800 | tf_op jit(solution)/shard_map/while | solution.py:91
  176.7 75.0 %while.13 = (s32[]{:T(128)}, f32[4,2,4,128]{3,2,1,0:T(4,128)S(1)}, f32[4,4,128]{2,1,0:T(4,128)S(1)}, s32[4]{0:T(128)S(1)}, s32[]{:T(128)}, /*index=5*/bf16[48,2,20,2560]{3,2,1,0:T(8,128)(2,1)}, s32[4]{0:T(128)S(1)}) while((s32[]{:T(128)}, f32[4,2,4,128]{3,2,1,0:T(4,128)S(1)}, f32[4,4,128]{2,1,0:T(4,128)S(1)}, s32[4]{0:T(128)S(1)}, ...), condition=%wide.region_1.2_spmd.clone, body=%wide.region_0.1_spmd.sunk.clone | while | flops 81596248 | bytes 7054617 | solution.py:91
  180.4 1.3 collective-permute-start
  181.7 4.0 %collective-permute-start.1 = (bf16[2,2,3,2560]{3,2,1,0:T(4,128)(2,1)S(1)}, bf16[2,2,3,2560]{3,2,1,0:T(4,128)(2,1)S(1)}, u32[]{:S(2)}, u32[]{:S(2)}) collective-permute-start(bf16[2,2,3,2560]{3,2,1,0:T(4,128)(2,1)S(1)} %get-tuple-element.159), channel_id=1, source_target_pairs={{0,2},{1,3},{4,6},{5,7},{8,10},{9,11},{12,14},{13,15},{16,18},{17,... | collective-permute-start | bytes 184328 | tf_op jit(solution)/shard_map/while/body/eval_jaxpr/ppermute | solution.py:14
  185.7 1.4 collective-permute-done.1
  187.5 1.3 collective-permute-start.2
  188.8 3.5 %collective-permute-start.3 = (bf16[2,2,26,11]{3,2,1,0:T(8,128)(2,1)S(1)}, bf16[2,2,26,11]{3,2,1,0:T(8,128)(2,1)S(1)}, u32[]{:S(2)}, u32[]{:S(2)}) collective-permute-start(bf16[2,2,26,11]{3,2,1,0:T(8,128)(2,1)S(1)} %get-tuple-element.161), channel_id=1, source_target_pairs={{1,0},{3,2},{5,4},{7,6},{9,8},{11,10},{13,12},{15,14},{17,16},{19,... | collective-permute-start | bytes 6872 | tf_op jit(solution)/shard_map/while/body/eval_jaxpr/ppermute | solution.py:15
  199.2 1.3 collective-permute-start
  200.5 4.0 %collective-permute-start.1 = (bf16[2,2,3,2560]{3,2,1,0:T(4,128)(2,1)S(1)}, bf16[2,2,3,2560]{3,2,1,0:T(4,128)(2,1)S(1)}, u32[]{:S(2)}, u32[]{:S(2)}) collective-permute-start(bf16[2,2,3,2560]{3,2,1,0:T(4,128)(2,1)S(1)} %get-tuple-element.159), channel_id=1, source_target_pairs={{0,2},{1,3},{4,6},{5,7},{8,10},{9,11},{12,14},{13,15},{16,18},{17,... | collective-permute-start | bytes 184328 | tf_op jit(solution)/shard_map/while/body/eval_jaxpr/ppermute | solution.py:14
  206.4 1.3 collective-permute-start.2
  207.7 3.4 %collective-permute-start.3 = (bf16[2,2,26,11]{3,2,1,0:T(8,128)(2,1)S(1)}, bf16[2,2,26,11]{3,2,1,0:T(8,128)(2,1)S(1)}, u32[]{:S(2)}, u32[]{:S(2)}) collective-permute-start(bf16[2,2,26,11]{3,2,1,0:T(8,128)(2,1)S(1)} %get-tuple-element.161), channel_id=1, source_target_pairs={{1,0},{3,2},{5,4},{7,6},{9,8},{11,10},{13,12},{15,14},{17,16},{19,... | collective-permute-start | bytes 6872 | tf_op jit(solution)/shard_map/while/body/eval_jaxpr/ppermute | solution.py:15
  217.9 1.3 collective-permute-start
  219.2 4.0 %collective-permute-start.1 = (bf16[2,2,3,2560]{3,2,1,0:T(4,128)(2,1)S(1)}, bf16[2,2,3,2560]{3,2,1,0:T(4,128)(2,1)S(1)}, u32[]{:S(2)}, u32[]{:S(2)}) collective-permute-start(bf16[2,2,3,2560]{3,2,1,0:T(4,128)(2,1)S(1)} %get-tuple-element.159), channel_id=1, source_target_pairs={{0,2},{1,3},{4,6},{5,7},{8,10},{9,11},{12,14},{13,15},{16,18},{17,... | collective-permute-start | bytes 184328 | tf_op jit(solution)/shard_map/while/body/eval_jaxpr/ppermute | solution.py:14
  225.1 1.3 collective-permute-start.2
  226.4 3.4 %collective-permute-start.3 = (bf16[2,2,26,11]{3,2,1,0:T(8,128)(2,1)S(1)}, bf16[2,2,26,11]{3,2,1,0:T(8,128)(2,1)S(1)}, u32[]{:S(2)}, u32[]{:S(2)}) collective-permute-start(bf16[2,2,26,11]{3,2,1,0:T(8,128)(2,1)S(1)} %get-tuple-element.161), channel_id=1, source_target_pairs={{1,0},{3,2},{5,4},{7,6},{9,8},{11,10},{13,12},{15,14},{17,16},{19,... | collective-permute-start | bytes 6872 | tf_op jit(solution)/shard_map/while/body/eval_jaxpr/ppermute | solution.py:15
  236.7 1.3 collective-permute-start
  238.0 4.0 %collective-permute-start.1 = (bf16[2,2,3,2560]{3,2,1,0:T(4,128)(2,1)S(1)}, bf16[2,2,3,2560]{3,2,1,0:T(4,128)(2,1)S(1)}, u32[]{:S(2)}, u32[]{:S(2)}) collective-permute-start(bf16[2,2,3,2560]{3,2,1,0:T(4,128)(2,1)S(1)} %get-tuple-element.159), channel_id=1, source_target_pairs={{0,2},{1,3},{4,6},{5,7},{8,10},{9,11},{12,14},{13,15},{16,18},{17,... | collective-permute-start | bytes 184328 | tf_op jit(solution)/shard_map/while/body/eval_jaxpr/ppermute | solution.py:14
  243.8 1.3 collective-permute-start.2
  245.1 3.4 %collective-permute-start.3 = (bf16[2,2,26,11]{3,2,1,0:T(8,128)(2,1)S(1)}, bf16[2,2,26,11]{3,2,1,0:T(8,128)(2,1)S(1)}, u32[]{:S(2)}, u32[]{:S(2)}) collective-permute-start(bf16[2,2,26,11]{3,2,1,0:T(8,128)(2,1)S(1)} %get-tuple-element.161), channel_id=1, source_target_pairs={{1,0},{3,2},{5,4},{7,6},{9,8},{11,10},{13,12},{15,14},{17,16},{19,... | collective-permute-start | bytes 6872 | tf_op jit(solution)/shard_map/while/body/eval_jaxpr/ppermute | solution.py:15
  (81 shorter events, 30.5 us)
Async XLA Ops:
  3.5 145.3 %collective-permute-start.4 = (bf16[16,2,20,2560]{3,0,2,1:T(8,128)(2,1)S(1)}, bf16[16,2,20,2560]{3,0,2,1:T(8,128)(2,1)}, u32[]{:S(2)}, u32[]{:S(2)}) collective-permute-start(bf16[16,2,20,2560]{3,0,2,1:T(8,128)(2,1)S(1)} %copy.9), channel_id=1, source_target_pairs={{0,4},{4,8},{8,12},{12,16},{16,20},{20,24},{24,28},{28,32},{32,36}... | collective-permute-start | bytes 9830408 | tf_op jit(solution)/shard_map/ppermute | solution.py:14
  10.7 145.3 %collective-permute-start.5 = (bf16[16,2,20,2560]{3,0,2,1:T(8,128)(2,1)S(1)}, bf16[16,2,20,2560]{3,0,2,1:T(8,128)(2,1)}, u32[]{:S(2)}, u32[]{:S(2)}) collective-permute-start(bf16[16,2,20,2560]{3,0,2,1:T(8,128)(2,1)S(1)} %copy.9), channel_id=1, source_target_pairs={{4,0},{8,4},{12,8},{16,12},{20,16},{24,20},{28,24},{32,28},{36,32}... | collective-permute-start | bytes 9830408 | tf_op jit(solution)/shard_map/ppermute | solution.py:15
  160.5 16.2 %copy-start = (s32[4]{0:T(128)S(1)}, s32[4]{0:T(128)}, u32[]{:S(2)}) copy-start(s32[4]{0:T(128)} %param.7) | copy-start | bytes 52
  160.5 16.2 %copy-start.1 = (s32[4]{0:T(128)S(1)}, s32[4]{0:T(128)}, u32[]{:S(2)}) copy-start(s32[4]{0:T(128)} %param.8) | copy-start | bytes 52
  180.4 5.3 %collective-permute-start = (bf16[2,2,3,2560]{3,2,1,0:T(4,128)(2,1)S(1)}, bf16[2,2,3,2560]{3,2,1,0:T(4,128)(2,1)S(1)}, u32[]{:S(2)}, u32[]{:S(2)}) collective-permute-start(bf16[2,2,3,2560]{3,2,1,0:T(4,128)(2,1)S(1)} %get-tuple-element.158), channel_id=1, source_target_pairs={{2,0},{3,1},{6,4},{7,5},{10,8},{11,9},{14,12},{15,13},{18,16},{19,... | collective-permute-start | bytes 184328 | tf_op jit(solution)/shard_map/while/body/eval_jaxpr/ppermute | solution.py:15
  181.7 5.5 %collective-permute-start.1 = (bf16[2,2,3,2560]{3,2,1,0:T(4,128)(2,1)S(1)}, bf16[2,2,3,2560]{3,2,1,0:T(4,128)(2,1)S(1)}, u32[]{:S(2)}, u32[]{:S(2)}) collective-permute-start(bf16[2,2,3,2560]{3,2,1,0:T(4,128)(2,1)S(1)} %get-tuple-element.159), channel_id=1, source_target_pairs={{0,2},{1,3},{4,6},{5,7},{8,10},{9,11},{12,14},{13,15},{16,18},{17,... | collective-permute-start | bytes 184328 | tf_op jit(solution)/shard_map/while/body/eval_jaxpr/ppermute | solution.py:14
  187.5 4.9 %collective-permute-start.2 = (bf16[2,2,26,11]{3,2,1,0:T(8,128)(2,1)S(1)}, bf16[2,2,26,11]{3,2,1,0:T(8,128)(2,1)S(1)}, u32[]{:S(2)}, u32[]{:S(2)}) collective-permute-start(bf16[2,2,26,11]{3,2,1,0:T(8,128)(2,1)S(1)} %get-tuple-element.160), channel_id=1, source_target_pairs={{0,1},{2,3},{4,5},{6,7},{8,9},{10,11},{12,13},{14,15},{16,17},{18,... | collective-permute-start | bytes 6872 | tf_op jit(solution)/shard_map/while/body/eval_jaxpr/ppermute | solution.py:14
  188.8 4.4 %collective-permute-start.3 = (bf16[2,2,26,11]{3,2,1,0:T(8,128)(2,1)S(1)}, bf16[2,2,26,11]{3,2,1,0:T(8,128)(2,1)S(1)}, u32[]{:S(2)}, u32[]{:S(2)}) collective-permute-start(bf16[2,2,26,11]{3,2,1,0:T(8,128)(2,1)S(1)} %get-tuple-element.161), channel_id=1, source_target_pairs={{1,0},{3,2},{5,4},{7,6},{9,8},{11,10},{13,12},{15,14},{17,16},{19,... | collective-permute-start | bytes 6872 | tf_op jit(solution)/shard_map/while/body/eval_jaxpr/ppermute | solution.py:15
  199.2 5.6 %collective-permute-start = (bf16[2,2,3,2560]{3,2,1,0:T(4,128)(2,1)S(1)}, bf16[2,2,3,2560]{3,2,1,0:T(4,128)(2,1)S(1)}, u32[]{:S(2)}, u32[]{:S(2)}) collective-permute-start(bf16[2,2,3,2560]{3,2,1,0:T(4,128)(2,1)S(1)} %get-tuple-element.158), channel_id=1, source_target_pairs={{2,0},{3,1},{6,4},{7,5},{10,8},{11,9},{14,12},{15,13},{18,16},{19,... | collective-permute-start | bytes 184328 | tf_op jit(solution)/shard_map/while/body/eval_jaxpr/ppermute | solution.py:15
  200.5 5.5 %collective-permute-start.1 = (bf16[2,2,3,2560]{3,2,1,0:T(4,128)(2,1)S(1)}, bf16[2,2,3,2560]{3,2,1,0:T(4,128)(2,1)S(1)}, u32[]{:S(2)}, u32[]{:S(2)}) collective-permute-start(bf16[2,2,3,2560]{3,2,1,0:T(4,128)(2,1)S(1)} %get-tuple-element.159), channel_id=1, source_target_pairs={{0,2},{1,3},{4,6},{5,7},{8,10},{9,11},{12,14},{13,15},{16,18},{17,... | collective-permute-start | bytes 184328 | tf_op jit(solution)/shard_map/while/body/eval_jaxpr/ppermute | solution.py:14
  206.4 4.7 %collective-permute-start.2 = (bf16[2,2,26,11]{3,2,1,0:T(8,128)(2,1)S(1)}, bf16[2,2,26,11]{3,2,1,0:T(8,128)(2,1)S(1)}, u32[]{:S(2)}, u32[]{:S(2)}) collective-permute-start(bf16[2,2,26,11]{3,2,1,0:T(8,128)(2,1)S(1)} %get-tuple-element.160), channel_id=1, source_target_pairs={{0,1},{2,3},{4,5},{6,7},{8,9},{10,11},{12,13},{14,15},{16,17},{18,... | collective-permute-start | bytes 6872 | tf_op jit(solution)/shard_map/while/body/eval_jaxpr/ppermute | solution.py:14
  207.7 4.2 %collective-permute-start.3 = (bf16[2,2,26,11]{3,2,1,0:T(8,128)(2,1)S(1)}, bf16[2,2,26,11]{3,2,1,0:T(8,128)(2,1)S(1)}, u32[]{:S(2)}, u32[]{:S(2)}) collective-permute-start(bf16[2,2,26,11]{3,2,1,0:T(8,128)(2,1)S(1)} %get-tuple-element.161), channel_id=1, source_target_pairs={{1,0},{3,2},{5,4},{7,6},{9,8},{11,10},{13,12},{15,14},{17,16},{19,... | collective-permute-start | bytes 6872 | tf_op jit(solution)/shard_map/while/body/eval_jaxpr/ppermute | solution.py:15
  217.9 5.6 %collective-permute-start = (bf16[2,2,3,2560]{3,2,1,0:T(4,128)(2,1)S(1)}, bf16[2,2,3,2560]{3,2,1,0:T(4,128)(2,1)S(1)}, u32[]{:S(2)}, u32[]{:S(2)}) collective-permute-start(bf16[2,2,3,2560]{3,2,1,0:T(4,128)(2,1)S(1)} %get-tuple-element.158), channel_id=1, source_target_pairs={{2,0},{3,1},{6,4},{7,5},{10,8},{11,9},{14,12},{15,13},{18,16},{19,... | collective-permute-start | bytes 184328 | tf_op jit(solution)/shard_map/while/body/eval_jaxpr/ppermute | solution.py:15
  219.2 5.5 %collective-permute-start.1 = (bf16[2,2,3,2560]{3,2,1,0:T(4,128)(2,1)S(1)}, bf16[2,2,3,2560]{3,2,1,0:T(4,128)(2,1)S(1)}, u32[]{:S(2)}, u32[]{:S(2)}) collective-permute-start(bf16[2,2,3,2560]{3,2,1,0:T(4,128)(2,1)S(1)} %get-tuple-element.159), channel_id=1, source_target_pairs={{0,2},{1,3},{4,6},{5,7},{8,10},{9,11},{12,14},{13,15},{16,18},{17,... | collective-permute-start | bytes 184328 | tf_op jit(solution)/shard_map/while/body/eval_jaxpr/ppermute | solution.py:14
  225.1 4.7 %collective-permute-start.2 = (bf16[2,2,26,11]{3,2,1,0:T(8,128)(2,1)S(1)}, bf16[2,2,26,11]{3,2,1,0:T(8,128)(2,1)S(1)}, u32[]{:S(2)}, u32[]{:S(2)}) collective-permute-start(bf16[2,2,26,11]{3,2,1,0:T(8,128)(2,1)S(1)} %get-tuple-element.160), channel_id=1, source_target_pairs={{0,1},{2,3},{4,5},{6,7},{8,9},{10,11},{12,13},{14,15},{16,17},{18,... | collective-permute-start | bytes 6872 | tf_op jit(solution)/shard_map/while/body/eval_jaxpr/ppermute | solution.py:14
  226.4 4.2 %collective-permute-start.3 = (bf16[2,2,26,11]{3,2,1,0:T(8,128)(2,1)S(1)}, bf16[2,2,26,11]{3,2,1,0:T(8,128)(2,1)S(1)}, u32[]{:S(2)}, u32[]{:S(2)}) collective-permute-start(bf16[2,2,26,11]{3,2,1,0:T(8,128)(2,1)S(1)} %get-tuple-element.161), channel_id=1, source_target_pairs={{1,0},{3,2},{5,4},{7,6},{9,8},{11,10},{13,12},{15,14},{17,16},{19,... | collective-permute-start | bytes 6872 | tf_op jit(solution)/shard_map/while/body/eval_jaxpr/ppermute | solution.py:15
  236.7 5.6 %collective-permute-start = (bf16[2,2,3,2560]{3,2,1,0:T(4,128)(2,1)S(1)}, bf16[2,2,3,2560]{3,2,1,0:T(4,128)(2,1)S(1)}, u32[]{:S(2)}, u32[]{:S(2)}) collective-permute-start(bf16[2,2,3,2560]{3,2,1,0:T(4,128)(2,1)S(1)} %get-tuple-element.158), channel_id=1, source_target_pairs={{2,0},{3,1},{6,4},{7,5},{10,8},{11,9},{14,12},{15,13},{18,16},{19,... | collective-permute-start | bytes 184328 | tf_op jit(solution)/shard_map/while/body/eval_jaxpr/ppermute | solution.py:15
  238.0 5.5 %collective-permute-start.1 = (bf16[2,2,3,2560]{3,2,1,0:T(4,128)(2,1)S(1)}, bf16[2,2,3,2560]{3,2,1,0:T(4,128)(2,1)S(1)}, u32[]{:S(2)}, u32[]{:S(2)}) collective-permute-start(bf16[2,2,3,2560]{3,2,1,0:T(4,128)(2,1)S(1)} %get-tuple-element.159), channel_id=1, source_target_pairs={{0,2},{1,3},{4,6},{5,7},{8,10},{9,11},{12,14},{13,15},{16,18},{17,... | collective-permute-start | bytes 184328 | tf_op jit(solution)/shard_map/while/body/eval_jaxpr/ppermute | solution.py:14
  243.8 4.7 %collective-permute-start.2 = (bf16[2,2,26,11]{3,2,1,0:T(8,128)(2,1)S(1)}, bf16[2,2,26,11]{3,2,1,0:T(8,128)(2,1)S(1)}, u32[]{:S(2)}, u32[]{:S(2)}) collective-permute-start(bf16[2,2,26,11]{3,2,1,0:T(8,128)(2,1)S(1)} %get-tuple-element.160), channel_id=1, source_target_pairs={{0,1},{2,3},{4,5},{6,7},{8,9},{10,11},{12,13},{14,15},{16,17},{18,... | collective-permute-start | bytes 6872 | tf_op jit(solution)/shard_map/while/body/eval_jaxpr/ppermute | solution.py:14
  245.1 4.2 %collective-permute-start.3 = (bf16[2,2,26,11]{3,2,1,0:T(8,128)(2,1)S(1)}, bf16[2,2,26,11]{3,2,1,0:T(8,128)(2,1)S(1)}, u32[]{:S(2)}, u32[]{:S(2)}) collective-permute-start(bf16[2,2,26,11]{3,2,1,0:T(8,128)(2,1)S(1)} %get-tuple-element.161), channel_id=1, source_target_pairs={{1,0},{3,2},{5,4},{7,6},{9,8},{11,10},{13,12},{15,14},{17,16},{19,... | collective-permute-start | bytes 6872 | tf_op jit(solution)/shard_map/while/body/eval_jaxpr/ppermute | solution.py:15
where the time goes:
time: 254 us; the launch traced here: 253 us
  waiting for transfers between devices  152 us (60%)
  starting transfers between devices  48.5 us (19%)
  local copies, waits for them, and re-layouts  31.5 us (12%)
  other arithmetic  8.17 us (3%)
  loops' own time  5.72 us (2%)
  matrix products  5.47 us (2%)
    ppermute x9, waiting for transfers between devices, with_halo(): before = lax.ppermute(last, axis, up)  141 us
    ppermute x9, starting transfers between devices, with_halo(): before = lax.ppermute(last, axis, up)  28.4 us
    ppermute x9, starting transfers between devices, with_halo(): after = lax.ppermute(leading, axis, down)  20.1 us
    while x1, local copies, waits for them, and re-layouts, on_device(): lax.map(one_pair, (slots, reference_index, secondary_index))  16.2 us
    ppermute x9, waiting for transfers between devices, with_halo(): after = lax.ppermute(leading, axis, down)  11.2 us
    another operation x1, loops' own time, on_device(): lax.map(one_pair, (slots, reference_index, secondary_index))  5.72 us
    concatenate x5, other arithmetic, with_halo(): array = jnp.concatenate([before, array, after], axis=dim)  5.59 us
  transfers between devices with their start and end apart: 18, of which 13 were waited for; matrix products, arithmetic and copies ran while one was open for 0% of the time, Pallas kernels for 0%

commit v1 on v0

v1 whole, which is shorter than its diff:
```python
import jax
import jax.numpy as jnp
from jax import lax
from jax.experimental import pallas as pl
from jax.experimental.layout import Layout, with_layout_constraint
from jax.experimental.pallas import tpu as pltpu
from jax.sharding import PartitionSpec as P

MESH = pl.DeviceIdType.MESH
ACQ = 16
SLOTS = 4
LINES = 20
TILES = 20
WIDE = TILES + 1
EDGE = 3
COMBOS = ((13, 0), (14, 0), (15, 0), (14, 1), (15, 1), (15, 2))
CROSS = 2 * 3 * SLOTS
EARLY = CROSS + ACQ
LATE = 2 * len(COMBOS)
PITCH = 24
ROWS = LINES * WIDE * 2
F32 = jnp.float32
BF16 = jnp.bfloat16


def kernel(
    acq, ref_hbm, sec_hbm, cnt_hbm, ifg, coh,
    block, edge, relay_a, relay_b, wide, wide_edge, table,
    sums, lhs, early, late,
    out_a, out_b, in_a, in_b,
    ref_own, sec_own, ref_prev, sec_prev, ref_next, sec_next, count,
    local_sem, slab_send, relay_recv, pass_send, edge_recv,
    tile_send, tile_recv, index_send, index_recv, back_send, back_recv,
):
    d = lax.axis_index("pair")
    az = lax.axis_index("az")
    rg = lax.axis_index("rg")
    n = lax.axis_size("pair")
    oaz = 1 - az
    org = 1 - rg

    def at(step):
        return lax.rem(d + step + n, n)

    prev, nxt = at(-1), at(1)
    twin = d + 1 - 2 * lax.rem(d, 2)
    first = base = ACQ * d
    upper = az == 0

    own = [
        pltpu.make_async_copy(acq, block.at[:, :, pl.ds(0, TILES)], local_sem.at[0]),
        pltpu.make_async_copy(ref_hbm, ref_own, local_sem.at[1]),
        pltpu.make_async_copy(sec_hbm, sec_own, local_sem.at[2]),
        pltpu.make_async_copy(cnt_hbm, count, local_sem.at[3]),
    ]
    for copy in own:
        copy.start()

    barrier = pltpu.get_barrier_semaphore()
    peers = [
        (d, az, org), (d, oaz, rg),
        (prev, az, rg), (nxt, az, rg),
        (prev, az, org), (nxt, az, org),
        (prev, oaz, rg), (nxt, oaz, rg),
        (at(-2), oaz, rg), (at(2), oaz, rg),
    ]
    for peer in peers:
        pl.semaphore_signal(barrier, inc=1, device_id=peer, device_id_type=MESH)

    col = lax.broadcasted_iota(jnp.int32, (128, 128), 1) * 20
    row = lax.broadcasted_iota(jnp.int32, (128, 128), 0)
    for t in range(WIDE):
        sample = row + 128 * t
        if t == TILES:
            sample = sample - (128 * WIDE) * rg
        inside = (sample >= col - 10) & (sample <= col + 30)
        table[pl.ds(128 * t, 128), :] = jnp.where(inside, 1.0, 0.0).astype(BF16)

    pl.semaphore_wait(barrier, len(peers))

    def remote(src, dst, send, recv, device):
        return pltpu.make_async_remote_copy(
            src_ref=src, dst_ref=dst, send_sem=send, recv_sem=recv,
            device_id=device, device_id_type=MESH,
        )

    half = LINES // 2
    slabs = []
    for a in range(EDGE):
        slabs.append((
            remote(acq.at[a, pl.ds(0, half)], relay_a.at[a],
                   slab_send.at[a, 0], relay_recv.at[a, 0], (d, oaz, rg)),
            remote(acq.at[a, pl.ds(half, half)], relay_b.at[a],
                   slab_send.at[a, 1], relay_recv.at[a, 1], (twin, oaz, rg)),
        ))
    border = (TILES - 1) * org
    tiles = [
        remote(acq.at[:, :, border], block.at[:, :, TILES],
               tile_send.at[0], tile_recv.at[0], (d, az, org)),
        remote(acq.at[pl.ds(0, EDGE), :, border], edge.at[:, :, TILES],
               tile_send.at[1], tile_recv.at[1], (prev, az, org)),
    ]
    indices = [
        remote(ref_hbm, ref_next, index_send.at[0], index_recv.at[0], (prev, az, rg)),
        remote(sec_hbm, sec_next, index_send.at[1], index_recv.at[1], (prev, az, rg)),
        remote(ref_hbm, ref_prev, index_send.at[2], index_recv.at[2], (nxt, az, rg)),
        remote(sec_hbm, sec_prev, index_send.at[3], index_recv.at[3], (nxt, az, rg)),
    ]
    tiles[0].start()
    for copy in indices:
        copy.start()
    for pair in slabs:
        for copy in pair:
            copy.start()
    tiles[1].start()

    passes = []
    twin_prev = lax.rem(twin - 1 + n, n)
    for a in range(EDGE):
        passes.append((
            remote(relay_a.at[a], edge.at[a, pl.ds(0, half), pl.ds(0, TILES)],
                   pass_send.at[a, 0], edge_recv.at[a, 0], (prev, oaz, rg)),
            remote(relay_b.at[a], edge.at[a, pl.ds(half, half), pl.ds(0, TILES)],
                   pass_send.at[a, 1], edge_recv.at[a, 1], (twin_prev, oaz, rg)),
        ))

    def relay(a):
        for h in range(2):
            slabs[a][h].wait_recv()
            passes[a][h].start()

    def line(ref, a, l):
        start = a * ROWS + l * (2 * WIDE)
        return (
            ref[pl.ds(start, WIDE, stride=2), :],
            ref[pl.ds(start + 1, WIDE, stride=2), :],
        )

    def put(plane, window, value):
        start = pl.multiple_of((plane * 8 + window) * PITCH, 8)
        sums[pl.ds(start, WIDE), :] = value

    def line_sums(plane, get):
        def add(*terms):
            total = terms[0]
            for term in terms[1:]:
                total = tuple(x + y for x, y in zip(total, term))
            return total

        def store(window, value):
            for i, v in enumerate(value):
                put(plane + i, window, v)

        l2 = None
        s0 = add(get(0), get(1))
        l2 = get(2)
        up = add(s0, l2)
        s3 = add(get(3), get(4), get(5), get(6))
        l7 = get(7)
        m1 = add(s3, l7)
        store(0, add(up, m1))
        s8 = add(get(8), get(9), get(10), get(11))
        l12 = get(12)
        m2 = add(s8, l12)
        store(1, add(l2, m1, m2))
        s13 = add(get(13), get(14), get(15), get(16))
        l17 = get(17)
        m3 = add(s13, l17)
        store(2, add(l7, m2, m3))
        down = add(l17, get(18), get(19))
        store(3, add(l12, s13, down))
        store(4, tuple(jnp.where(upper, x, y) for x, y in zip(down, up)))

    def power(plane, a):
        def get(l):
            x, y = line(wide, a, l)
            return (x * x + y * y,)
        line_sums(plane, get)

    def cross(plane, a, other, b):
        def get(l):
            xr, yr = line(wide, a, l)
            xs, ys = line(other, b, l)
            return (xr * xs + yr * ys, yr * xs - xr * ys)
        line_sums(plane, get)

    def range_sums(planes, result):
        rows = planes * 8
        for t in range(WIDE):
            v = sums[pl.ds(t, rows, stride=PITCH), :]
            hi = v.astype(BF16)
            lo = (v - hi.astype(F32)).astype(BF16)
            lhs[pl.ds(0, rows), pl.ds(128 * t, 128)] = hi
            lhs[pl.ds(rows, rows), pl.ds(128 * t, 128)] = lo
        both = jnp.dot(lhs[pl.ds(0, 2 * rows), :], table[...], preferred_element_type=F32)
        total = both[:rows] + both[rows:]
        result[...] = total.reshape(planes, 8, 128)

    own[0].wait()
    tiles[0].wait_recv()

    def widen(a, carry):
        start = pl.multiple_of(a * ROWS, 8)
        wide[pl.ds(start, ROWS), :] = block[a].reshape(ROWS, 128).astype(F32)
        return carry

    lax.fori_loop(0, ACQ, widen, 0)

    def power_step(a, carry):
        power(CROSS + a, a)
        return carry

    lax.fori_loop(0, ACQ, power_step, 0)
    relay(0)

    for copy in own[1:]:
        copy.wait()
    for copy in indices:
        copy.wait_recv()
    names = [(ref_prev, sec_prev), (ref_own, sec_own), (ref_next, sec_next)]

    def clip(i):
        return jnp.clip(i, 0, ACQ - 1)

    for g, (refs, secs) in enumerate(names):
        def cross_step(k, carry, g=g, refs=refs, secs=secs):
            cross(2 * (SLOTS * g + k), clip(refs[k] - base), wide, clip(secs[k] - base))
            return carry
        lax.fori_loop(0, SLOTS, cross_step, 0)
        if g == 1:
            relay(1)

    range_sums(EARLY, early)
    relay(2)

    tiles[1].wait_recv()
    done = 0
    for a in range(EDGE):
        for h in range(2):
            passes[a][h].wait_recv()
        wide_edge[pl.ds(a * ROWS, ROWS), :] = edge[a].reshape(ROWS, 128).astype(F32)
        for i, (r, s) in enumerate(COMBOS):
            if s == a:
                cross(2 * i, r, wide_edge, s)
    range_sums(LATE, late)

    zero = jnp.zeros((8, 128), F32)
    for g, (refs, secs) in enumerate(names):
        for k in range(SLOTS):
            r = refs[k] - base
            s = secs[k] - base
            has_r = (r >= 0) & (r < ACQ)
            has_s = (s >= 0) & (s < ACQ)
            inner = has_r & (s < ACQ)
            outer = has_r & (s >= ACQ)
            combo = jnp.where(s == ACQ, r - 13, jnp.where(s == ACQ + 1, r - 11, 5))
            combo = jnp.clip(combo, 0, len(COMBOS) - 1)
            for c in range(4):
                if c < 2:
                    value = jnp.where(inner, early[2 * (SLOTS * g + k) + c], zero)
                    if g > 0:
                        value = value + jnp.where(outer, late[2 * combo + c], zero)
                elif c == 2:
                    value = jnp.where(has_r, early[CROSS + clip(r)], zero)
                else:
                    value = jnp.where(has_s, early[CROSS + clip(s)], zero)
                out_a[g, 4 * k + c] = value[0:4]
                out_b[g, pl.ds(4 * k + c, 1), :] = value[4:5]

    backs = [
        remote(out_b.at[1], in_b.at[1], back_send.at[3], back_recv.at[3], (d, oaz, rg)),
        remote(out_a.at[0], in_a.at[1], back_send.at[0], back_recv.at[0], (prev, az, rg)),
        remote(out_a.at[2], in_a.at[0], back_send.at[1], back_recv.at[1], (nxt, az, rg)),
        remote(out_b.at[0], in_b.at[2], back_send.at[2], back_recv.at[2], (prev, oaz, rg)),
        remote(out_b.at[2], in_b.at[0], back_send.at[4], back_recv.at[4], (nxt, oaz, rg)),
    ]
    for copy in backs:
        copy.start()
    for copy in tiles + indices:
        copy.wait_send()
    for a in range(EDGE):
        for h in range(2):
            slabs[a][h].wait_send()
            passes[a][h].wait_send()
    for copy in backs:
        copy.wait()

    window = lax.broadcasted_iota(jnp.int32, (4, 128), 0)
    shared = window == 3 * oaz
    for k in range(SLOTS):
        live = k < count[0]
        total = []
        for c in range(4):
            i = 4 * k + c
            rim = in_b[0, pl.ds(i, 1), :] + in_b[1, pl.ds(i, 1), :] + in_b[2, pl.ds(i, 1), :]
            body = out_a[1, i] + in_a[0, i] + in_a[1, i]
            total.append(body + jnp.where(shared, rim, 0.0))
        re, im, pr, ps = total
        none = jnp.zeros((4, 128), F32)
        ifg[k, 0] = jnp.where(live, re / 451.0, none)
        ifg[k, 1] = jnp.where(live, im / 451.0, none)
        value = jnp.sqrt(re * re + im * im) / jnp.sqrt(pr * ps + 1e-06)
        coh[k] = jnp.where(live, value, none)


def on_device(acquisitions, reference_index, secondary_index, pair_count):
    view = acquisitions.reshape(ACQ, 2, LINES, TILES, 128)
    view = with_layout_constraint(view, Layout((0, 2, 3, 1, 4)))
    view = view.transpose(0, 2, 3, 1, 4)
    hbm = pl.BlockSpec(memory_space=pl.ANY)
    vmem = pl.BlockSpec(memory_space=pltpu.VMEM)
    dma = pltpu.SemaphoreType.DMA
    return pl.pallas_call(
        kernel,
        out_shape=(
            jax.ShapeDtypeStruct((SLOTS, 2, 4, 128), F32),
            jax.ShapeDtypeStruct((SLOTS, 4, 128), F32),
        ),
        in_specs=[hbm] * 4,
        out_specs=(vmem, vmem),
        scratch_shapes=[
            pltpu.VMEM((ACQ, LINES, WIDE, 2, 128), BF16),
            pltpu.VMEM((EDGE, LINES, WIDE, 2, 128), BF16),
            pltpu.VMEM((EDGE, LINES // 2, TILES, 2, 128), BF16),
            pltpu.VMEM((EDGE, LINES // 2, TILES, 2, 128), BF16),
            pltpu.VMEM((ACQ * ROWS, 128), F32),
            pltpu.VMEM((EDGE * ROWS, 128), F32),
            pltpu.VMEM((128 * WIDE, 128), BF16),
            pltpu.VMEM((EARLY * 8 * PITCH, 128), F32),
            pltpu.VMEM((EARLY * 16, 128 * WIDE), BF16),
            pltpu.VMEM((EARLY, 8, 128), F32),
            pltpu.VMEM((LATE, 8, 128), F32),
            pltpu.VMEM((3, 16, 4, 128), F32),
            pltpu.VMEM((3, 16, 128), F32),
            pltpu.VMEM((2, 16, 4, 128), F32),
            pltpu.VMEM((3, 16, 128), F32),
        ] + [pltpu.SMEM((SLOTS,), jnp.int32)] * 6 + [pltpu.SMEM((1,), jnp.int32)] + [
            dma((4,)), dma((EDGE, 2)), dma((EDGE, 2)), dma((EDGE, 2)), dma((EDGE, 2)),
            dma((2,)), dma((2,)), dma((4,)), dma((4,)), dma((5,)), dma((5,)),
        ],
        compiler_params=pltpu.CompilerParams(
            collective_id=0, has_side_effects=True, vmem_limit_bytes=60 * 2**20
        ),
    )(view, reference_index, secondary_index, pair_count)


def solution(mesh):
    return jax.shard_map(
        on_device,
        mesh=mesh,
        in_specs=(P("pair", None, "az", "rg"), P("pair"), P("pair"), P("pair")),
        out_specs=(P("pair", None, "az", "rg"), P("pair", "az", "rg")),
        check_vma=False,
    )
```

time: 254 us -> 44.6 us (0.18)
  waiting for transfers between devices: 152 us -> 0 us
  starting transfers between devices: 48.5 us -> 0 us
  Pallas kernels: 0 us -> 40.4 us
  local copies, waits for them, and re-layouts: 31.5 us -> 2.62 us
  other arithmetic: 8.17 us -> 0 us
  loops' own time: 5.72 us -> 0 us
  matrix products: 5.47 us -> 0 us
    ppermute x18 -> x0, waiting for transfers between devices: 152 us -> none  [the longest x9 141 us: with_halo(): before = lax.ppermute(last, axis, up)]
    ppermute x18 -> x0, starting transfers between devices: 48.5 us -> none  [the longest x9 28.4 us: with_halo(): before = lax.ppermute(last, axis, up)]
    pallas_call x0 -> x1, Pallas kernels: none -> 40.4 us  [on_device(): pl.pallas_call(kernel, out_shape=(jax.ShapeDtypeStruct((SLOTS, 2, 4, 128)...]
    while x1 -> x0, local copies, waits for them, and re-layouts: 16.2 us -> none  [on_device(): lax.map(one_pair, (slots, reference_index, secondary_index))]
    dynamic_slice x12 -> x0, local copies, waits for them, and re-layouts: 9.1 us -> none  [the longest x8 4.7 us: on_device(): lax.map(one_pair, (slots, reference_index, secondary_index))]
    another operation x1 -> x0, loops' own time: 5.72 us -> none  [on_device(): lax.map(one_pair, (slots, reference_index, secondary_index))]
    concatenate x5 -> x0, other arithmetic: 5.59 us -> none  [with_halo(): array = jnp.concatenate([before, array, after], axis=dim)]
    dot_general x8 -> x0, matrix products: 5.47 us -> none  [the longest x4 2.79 us: window_sum(): jnp.einsum('cis,sj->cij', line_sums, sample_table, precision=lax.Precisio...]
  transfers between devices with their start and end apart: 18 -> 0, of which waited for: 13 -> 0; matrix products, arithmetic and copies ran while one was open for 0% -> 0% of each run, Pallas kernels for 0% -> 0%
where the time goes in v1:
time: 44.6 us; the launch traced here: 44.3 us
  Pallas kernels  40.4 us (91%)
  local copies, waits for them, and re-layouts  2.62 us (6%)
  between operations  1.29 us (3%)
    pallas_call x1, Pallas kernels, on_device(): pl.pallas_call(kernel, out_shape=(jax.ShapeDtypeStruct((SLOTS, 2, 4, 128)...  40.4 us
    unnamed x2, local copies, waits for them, and re-layouts  2.62 us

profile of v1, /device:TPU:1, one launch (start us, length us, event | category | flops | bytes accessed | tf_op | source)
XLA Modules:
  0.0 44.3 jit_solution(6207312114685803011)
XLA Ops:
  1.3 40.4 %shard_map.59 = (f32[4,2,4,128]{3,2,1,0:T(4,128)}, f32[4,4,128]{2,1,0:T(4,128)}) custom-call(bf16[16,20,20,2,128]{4,3,2,1,0:T(2,128)(2,1)} %bitcast.3, s32[4]{0:T(128)} %ref_hbm.1, s32[4]{0:T(128)} %sec_hbm.1, s32[1]{0:T(128)S(6)} %copy.8.cnt_hbm), custom_call_target="tpu_custom_call" | custom-call | tf_op jit(solution)/shard_map/pallas_call | solution.py:313
  41.7 1.3 %copy.9 = f32[4,2,4,128]{3,2,1,0:T(4,128)} copy(f32[4,2,4,128]{3,2,1,0:T(4,128)} %get-tuple-element.4) | data formatting | bytes 32768
  43.0 1.3 %copy.10 = f32[4,4,128]{2,1,0:T(4,128)} copy(f32[4,4,128]{2,1,0:T(4,128)} %get-tuple-element.5) | data formatting | bytes 16384

commit v2 on v1

v2 whole, which is shorter than its diff:
```python
import jax
import jax.numpy as jnp
from jax import lax
from jax.experimental import pallas as pl
from jax.experimental.layout import Layout, with_layout_constraint
from jax.experimental.pallas import tpu as pltpu
from jax.sharding import PartitionSpec as P

MESH = pl.DeviceIdType.MESH
ACQ = 16
SLOTS = 4
LINES = 20
TILES = 20
WIDE = TILES + 1
EDGE = 3
COMBOS = ((2, 0), (2, 1), (2, 2), (1, 0), (1, 1), (0, 0))
CROSS = 2 * 3 * SLOTS
EARLY = CROSS + ACQ
LATE = 2 * len(COMBOS)
PITCH = 24
ROWS = LINES * WIDE * 2
F32 = jnp.float32
BF16 = jnp.bfloat16


def kernel(
    acq, ref_hbm, sec_hbm, cnt_hbm, totals,
    block, edge, wide, wide_edge, table,
    sums, lhs, early, late,
    out_a, out_b, in_a, in_b, late_a, late_b, in_late_a, in_late_b,
    ref_own, sec_own, ref_prev, sec_prev, ref_next, sec_next, count,
    local_sem, slab_send, slab_recv,
    tile_send, tile_recv, index_send, index_recv, back_send, back_recv, late_send, late_recv,
):
    d = lax.axis_index("pair")
    az = lax.axis_index("az")
    rg = lax.axis_index("rg")
    n = lax.axis_size("pair")
    oaz = 1 - az
    org = 1 - rg

    def at(step):
        return lax.rem(d + step + n, n)

    prev, nxt = at(-1), at(1)
    base = ACQ * d
    upper = az == 0

    own = [
        pltpu.make_async_copy(acq, block.at[:, :, pl.ds(0, TILES)], local_sem.at[0]),
        pltpu.make_async_copy(ref_hbm, ref_own, local_sem.at[1]),
        pltpu.make_async_copy(sec_hbm, sec_own, local_sem.at[2]),
        pltpu.make_async_copy(cnt_hbm, count, local_sem.at[3]),
    ]
    for copy in own:
        copy.start()

    barrier = pltpu.get_barrier_semaphore()
    peers = [
        (d, az, org), (d, oaz, rg),
        (prev, az, rg), (nxt, az, rg),
        (prev, az, org), (nxt, az, org),
        (prev, oaz, rg), (nxt, oaz, rg),
    ]
    for peer in peers:
        pl.semaphore_signal(barrier, inc=1, device_id=peer, device_id_type=MESH)

    col = lax.broadcasted_iota(jnp.int32, (128, 128), 1) * 20
    row = lax.broadcasted_iota(jnp.int32, (128, 128), 0)
    for t in range(WIDE):
        sample = row + 128 * t
        if t == TILES:
            sample = sample - (128 * WIDE) * rg
        inside = (sample >= col - 10) & (sample <= col + 30)
        table[pl.ds(128 * t, 128), :] = jnp.where(inside, 1.0, 0.0).astype(BF16)

    pl.semaphore_wait(barrier, len(peers))

    def remote(src, dst, send, recv, device):
        return pltpu.make_async_remote_copy(
            src_ref=src, dst_ref=dst, send_sem=send, recv_sem=recv,
            device_id=device, device_id_type=MESH,
        )

    slabs = [
        remote(acq.at[ACQ - EDGE + a], edge.at[a, :, pl.ds(0, TILES)],
               slab_send.at[a], slab_recv.at[a], (nxt, az, rg))
        for a in range(EDGE)
    ]
    border = (TILES - 1) * org
    tiles = [
        remote(acq.at[:, :, border], block.at[:, :, TILES],
               tile_send.at[0], tile_recv.at[0], (d, az, org)),
        remote(acq.at[pl.ds(ACQ - EDGE, EDGE), :, border], edge.at[:, :, TILES],
               tile_send.at[1], tile_recv.at[1], (nxt, az, org)),
    ]
    indices = [
        remote(ref_hbm, ref_next, index_send.at[0], index_recv.at[0], (prev, az, rg)),
        remote(sec_hbm, sec_next, index_send.at[1], index_recv.at[1], (prev, az, rg)),
        remote(ref_hbm, ref_prev, index_send.at[2], index_recv.at[2], (nxt, az, rg)),
        remote(sec_hbm, sec_prev, index_send.at[3], index_recv.at[3], (nxt, az, rg)),
    ]
    for copy in indices:
        copy.start()
    for copy in tiles:
        copy.start()
    for a in (2, 1, 0):
        slabs[a].start()

    def line(ref, a, l):
        start = a * ROWS + l * (2 * WIDE)
        return (
            ref[pl.ds(start, WIDE, stride=2), :],
            ref[pl.ds(start + 1, WIDE, stride=2), :],
        )

    def put(plane, window, value):
        start = pl.multiple_of((plane * 8 + window) * PITCH, 8)
        sums[pl.ds(start, WIDE), :] = value

    def line_sums(plane, get):
        def add(*terms):
            total = terms[0]
            for term in terms[1:]:
                total = tuple(x + y for x, y in zip(total, term))
            return total

        def store(window, value):
            for i, v in enumerate(value):
                put(plane + i, window, v)

        l2 = None
        s0 = add(get(0), get(1))
        l2 = get(2)
        up = add(s0, l2)
        s3 = add(get(3), get(4), get(5), get(6))
        l7 = get(7)
        m1 = add(s3, l7)
        store(0, add(up, m1))
        s8 = add(get(8), get(9), get(10), get(11))
        l12 = get(12)
        m2 = add(s8, l12)
        store(1, add(l2, m1, m2))
        s13 = add(get(13), get(14), get(15), get(16))
        l17 = get(17)
        m3 = add(s13, l17)
        store(2, add(l7, m2, m3))
        down = add(l17, get(18), get(19))
        store(3, add(l12, s13, down))
        store(4, tuple(jnp.where(upper, x, y) for x, y in zip(down, up)))

    def power(plane, a):
        def get(l):
            x, y = line(wide, a, l)
            return (x * x + y * y,)
        line_sums(plane, get)

    def cross(plane, one, a, b):
        def get(l):
            xr, yr = line(one, a, l)
            xs, ys = line(wide, b, l)
            return (xr * xs + yr * ys, yr * xs - xr * ys)
        line_sums(plane, get)

    def range_sums(first, planes, result):
        rows = planes * 8
        for t in range(WIDE):
            v = sums[pl.ds(first * 8 * PITCH + t, rows, stride=PITCH), :]
            hi = v.astype(BF16)
            lo = (v - hi.astype(F32)).astype(BF16)
            lhs[pl.ds(0, rows), pl.ds(128 * t, 128)] = hi
            lhs[pl.ds(rows, rows), pl.ds(128 * t, 128)] = lo
        both = jnp.dot(lhs[pl.ds(0, 2 * rows), :], table[...], preferred_element_type=F32)
        total = both[:rows] + both[rows:]
        result[pl.ds(first, planes)] = total.reshape(planes, 8, 128)

    own[0].wait()
    tiles[0].wait_recv()

    def widen(a, carry):
        start = pl.multiple_of(a * ROWS, 8)
        wide[pl.ds(start, ROWS), :] = block[a].reshape(ROWS, 128).astype(F32)
        return carry

    lax.fori_loop(0, ACQ, widen, 0)

    def power_step(a, carry):
        power(CROSS + a, a)
        return carry

    lax.fori_loop(0, ACQ, power_step, 0)

    for copy in own[1:]:
        copy.wait()
    for copy in indices:
        copy.wait_recv()
    names = [(ref_prev, sec_prev), (ref_own, sec_own), (ref_next, sec_next)]

    def clip(i):
        return jnp.clip(i, 0, ACQ - 1)

    for g, (refs, secs) in enumerate(names):
        def cross_step(k, carry, g=g, refs=refs, secs=secs):
            cross(2 * (SLOTS * g + k), wide, clip(refs[k] - base), clip(secs[k] - base))
            return carry
        lax.fori_loop(0, SLOTS, cross_step, 0)

    range_sums(0, EARLY, early)

    zero = jnp.zeros((8, 128), F32)
    for g, (refs, secs) in enumerate(names):
        for k in range(SLOTS):
            r = refs[k] - base
            s = secs[k] - base
            has_r = (r >= 0) & (r < ACQ)
            has_s = (s >= 0) & (s < ACQ)
            for c in range(4):
                if c < 2:
                    value = jnp.where(has_r & has_s, early[2 * (SLOTS * g + k) + c], zero)
                elif c == 2:
                    value = jnp.where(has_r, early[CROSS + clip(r)], zero)
                else:
                    value = jnp.where(has_s, early[CROSS + clip(s)], zero)
                out_a[g, 4 * k + c] = value[0:4]
                out_b[g, pl.ds(4 * k + c, 1), :] = value[4:5]

    backs = [
        remote(out_a.at[2], in_a.at[0], back_send.at[1], back_recv.at[1], (nxt, az, rg)),
        remote(out_b.at[2], in_b.at[0], back_send.at[4], back_recv.at[4], (nxt, oaz, rg)),
        remote(out_a.at[0], in_a.at[1], back_send.at[0], back_recv.at[0], (prev, az, rg)),
        remote(out_b.at[0], in_b.at[2], back_send.at[2], back_recv.at[2], (prev, oaz, rg)),
        remote(out_b.at[1], in_b.at[1], back_send.at[3], back_recv.at[3], (d, oaz, rg)),
    ]
    for copy in backs:
        copy.start()

    tiles[1].wait_recv()
    for a in (2, 1, 0):
        slabs[a].wait_recv()
        wide_edge[pl.ds(a * ROWS, ROWS), :] = edge[a].reshape(ROWS, 128).astype(F32)
        for i, (r, s) in enumerate(COMBOS):
            if r == a:
                cross(2 * i, wide_edge, r, s)
        if a == 1:
            range_sums(0, 10, late)
    range_sums(10, 2, late)

    for g, (refs, secs) in enumerate(names[:2]):
        for k in range(SLOTS):
            r = refs[k] - base
            s = secs[k] - base
            reach = (r < 0) & (s >= 0) & (s < ACQ)
            combo = jnp.where(r == -1, s, jnp.where(r == -2, s + 3, 5))
            combo = jnp.clip(combo, 0, len(COMBOS) - 1)
            for c in range(2):
                value = jnp.where(reach, late[2 * combo + c], zero)
                late_a[g, 2 * k + c] = value[0:4]
                late_b[g, pl.ds(2 * k + c, 1), :] = value[4:5]

    lates = [
        remote(late_a.at[0], in_late_a, late_send.at[0], late_recv.at[0], (prev, az, rg)),
        remote(late_b.at[0], in_late_b.at[0], late_send.at[1], late_recv.at[1], (prev, oaz, rg)),
        remote(late_b.at[1], in_late_b.at[1], late_send.at[2], late_recv.at[2], (d, oaz, rg)),
    ]
    for copy in lates:
        copy.start()
    for copy in tiles + indices + slabs:
        copy.wait_send()
    for copy in backs + lates:
        copy.wait()

    window = lax.broadcasted_iota(jnp.int32, (4, 128), 0)
    shared = window == 3 * oaz
    for k in range(SLOTS):
        live = k < count[0]
        for c in range(4):
            i = 4 * k + c
            rim = in_b[0, pl.ds(i, 1), :] + in_b[1, pl.ds(i, 1), :] + in_b[2, pl.ds(i, 1), :]
            body = out_a[1, i] + in_a[0, i] + in_a[1, i]
            if c < 2:
                j = 2 * k + c
                rim = rim + in_late_b[0, pl.ds(j, 1), :] + in_late_b[1, pl.ds(j, 1), :]
                body = body + late_a[1, j] + in_late_a[j]
            total = body + jnp.where(shared, rim, 0.0)
            if c < 2:
                total = jnp.where(live, total, jnp.zeros((4, 128), F32))
            totals[k, c] = total


def finish(totals, ifg, coh):
    re, im = totals[:, 0], totals[:, 1]
    ifg[:, 0] = re / 451.0
    ifg[:, 1] = im / 451.0
    coh[...] = jnp.sqrt(re * re + im * im) / jnp.sqrt(totals[:, 2] * totals[:, 3] + 1e-06)


def on_device(acquisitions, reference_index, secondary_index, pair_count):
    view = acquisitions.reshape(ACQ, 2, LINES, TILES, 128)
    view = with_layout_constraint(view, Layout((0, 2, 3, 1, 4)))
    view = view.transpose(0, 2, 3, 1, 4)
    hbm = pl.BlockSpec(memory_space=pl.ANY)
    vmem = pl.BlockSpec(memory_space=pltpu.VMEM)
    dma = pltpu.SemaphoreType.DMA
    totals = pl.pallas_call(
        kernel,
        out_shape=jax.ShapeDtypeStruct((SLOTS, 4, 4, 128), F32),
        in_specs=[hbm] * 4,
        out_specs=vmem,
        scratch_shapes=[
            pltpu.VMEM((ACQ, LINES, WIDE, 2, 128), BF16),
            pltpu.VMEM((EDGE, LINES, WIDE, 2, 128), BF16),
            pltpu.VMEM((ACQ * ROWS, 128), F32),
            pltpu.VMEM((EDGE * ROWS, 128), F32),
            pltpu.VMEM((128 * WIDE, 128), BF16),
            pltpu.VMEM((EARLY * 8 * PITCH, 128), F32),
            pltpu.VMEM((EARLY * 16, 128 * WIDE), BF16),
            pltpu.VMEM((EARLY, 8, 128), F32),
            pltpu.VMEM((LATE, 8, 128), F32),
            pltpu.VMEM((3, 16, 4, 128), F32),
            pltpu.VMEM((3, 16, 128), F32),
            pltpu.VMEM((2, 16, 4, 128), F32),
            pltpu.VMEM((3, 16, 128), F32),
            pltpu.VMEM((2, 8, 4, 128), F32),
            pltpu.VMEM((2, 8, 128), F32),
            pltpu.VMEM((8, 4, 128), F32),
            pltpu.VMEM((2, 8, 128), F32),
        ] + [pltpu.SMEM((SLOTS,), jnp.int32)] * 6 + [pltpu.SMEM((1,), jnp.int32)] + [
            dma((4,)), dma((EDGE,)), dma((EDGE,)), dma((2,)), dma((2,)),
            dma((4,)), dma((4,)), dma((5,)), dma((5,)), dma((3,)), dma((3,)),
        ],
        compiler_params=pltpu.CompilerParams(
            collective_id=0, has_side_effects=True, vmem_limit_bytes=60 * 2**20
        ),
    )(view, reference_index, secondary_index, pair_count)
    return pl.pallas_call(
        finish,
        out_shape=(
            jax.ShapeDtypeStruct((SLOTS, 2, 4, 128), F32),
            jax.ShapeDtypeStruct((SLOTS, 4, 128), F32),
        ),
        in_specs=[vmem],
        out_specs=(vmem, vmem),
    )(totals)


def solution(mesh):
    return jax.shard_map(
        on_device,
        mesh=mesh,
        in_specs=(P("pair", None, "az", "rg"), P("pair"), P("pair"), P("pair")),
        out_specs=(P("pair", None, "az", "rg"), P("pair", "az", "rg")),
        check_vma=False,
    )
```

time: 44.6 us -> 36.5 us (0.82)
  Pallas kernels: 40.4 us -> 35.1 us
  local copies, waits for them, and re-layouts: 2.62 us -> 0 us
    pallas_call x1 -> x2, Pallas kernels: 40.4 us -> 35.1 us  [the longest x1 33.7 us: on_device(): pl.pallas_call(kernel, out_shape=jax.ShapeDtypeStruct((SLOTS, 4, 4, 128),...]
    unnamed x2 -> x0, local copies, waits for them, and re-layouts: 2.62 us -> none
where the time goes in v2:
time: 36.5 us; the launch traced here: 36.4 us
  Pallas kernels  35.1 us (96%)
  between operations  1.28 us (4%)
    pallas_call x1, Pallas kernels, on_device(): pl.pallas_call(kernel, out_shape=jax.ShapeDtypeStruct((SLOTS, 4, 4, 128),...  33.7 us
    pallas_call x1, Pallas kernels, on_device(): pl.pallas_call(finish, out_shape=(jax.ShapeDtypeStruct((SLOTS, 2, 4, 128)...  1.38 us

profile of v2, /device:TPU:1, one launch (start us, length us, event | category | flops | bytes accessed | tf_op | source)
XLA Modules:
  0.0 36.4 jit_solution(4116240927532692748)
XLA Ops:
  1.3 33.7 %shard_map.59.totals = f32[4,4,4,128]{3,2,1,0:T(4,128)} custom-call(bf16[16,20,20,2,128]{4,3,2,1,0:T(2,128)(2,1)} %bitcast.3, s32[4]{0:T(128)} %ref_hbm.1, s32[4]{0:T(128)} %sec_hbm.1, s32[1]{0:T(128)S(6)} %copy.6.cnt_hbm), custom_call_target="tpu_custom_call" | custom-call | tf_op jit(solution)/shard_map/pallas_call | solution.py:304
  35.0 1.4 %shard_map.60 = (f32[4,2,4,128]{3,2,1,0:T(4,128)}, f32[4,4,128]{2,1,0:T(4,128)}) custom-call(f32[4,4,4,128]{3,2,1,0:T(4,128)} %shard_map.59.totals), custom_call_target="tpu_custom_call" | custom-call | tf_op jit(solution)/shard_map/pallas_call | solution.py:335

commit v3 on v2

--- a/solution.py
+++ b/solution.py
@@ -24,13 +24,13 @@
 
 
 def kernel(
-    acq, ref_hbm, sec_hbm, cnt_hbm, totals,
+    acq, ref_hbm, sec_hbm, totals,
     block, edge, wide, wide_edge, table,
     sums, lhs, early, late,
     out_a, out_b, in_a, in_b, late_a, late_b, in_late_a, in_late_b,
-    ref_own, sec_own, ref_prev, sec_prev, ref_next, sec_next, count,
+    ref_own, sec_own, ref_prev, sec_prev, ref_next, sec_next,
     local_sem, slab_send, slab_recv,
-    tile_send, tile_recv, index_send, index_recv, back_send, back_recv, late_send, late_recv,
+    tile_send, tile_recv, index_send, index_recv, back_send, back_recv, late_send, late_recv, ready,
 ):
     d = lax.axis_index("pair")
     az = lax.axis_index("az")
@@ -50,7 +50,6 @@
         pltpu.make_async_copy(acq, block.at[:, :, pl.ds(0, TILES)], local_sem.at[0]),
         pltpu.make_async_copy(ref_hbm, ref_own, local_sem.at[1]),
         pltpu.make_async_copy(sec_hbm, sec_own, local_sem.at[2]),
-        pltpu.make_async_copy(cnt_hbm, count, local_sem.at[3]),
     ]
     for copy in own:
         copy.start()
@@ -58,12 +57,45 @@
     barrier = pltpu.get_barrier_semaphore()
     peers = [
         (d, az, org), (d, oaz, rg),
-        (prev, az, rg), (nxt, az, rg),
-        (prev, az, org), (nxt, az, org),
-        (prev, oaz, rg), (nxt, oaz, rg),
+        (prev, az, rg), (prev, az, org), (prev, oaz, rg),
     ]
     for peer in peers:
         pl.semaphore_signal(barrier, inc=1, device_id=peer, device_id_type=MESH)
+
+    pl.semaphore_wait(barrier, len(peers))
+    for peer in ((nxt, az, rg), (nxt, oaz, rg)):
+        pl.semaphore_signal(ready, inc=1, device_id=peer, device_id_type=MESH)
+
+    def remote(src, dst, send, recv, device):
+        return pltpu.make_async_remote_copy(
+            src_ref=src, dst_ref=dst, send_sem=send, recv_sem=recv,
+            device_id=device, device_id_type=MESH,
+        )
+
+    slabs = [
+        remote(acq.at[ACQ - EDGE + a], edge.at[a, :, pl.ds(0, TILES)],
+               slab_send.at[a], slab_recv.at[a], (nxt, az, rg))
+        for a in range(EDGE)
+    ]
+    border = (TILES - 1) * org
+    tiles = [
+        remote(acq.at[:, :, border], block.at[:, :, TILES],
+               tile_send.at[0], tile_recv.at[0], (d, az, org)),
+        remote(acq.at[pl.ds(ACQ - EDGE, EDGE), :, border], edge.at[:, :, TILES],
+               tile_send.at[1], tile_recv.at[1], (nxt, az, org)),
+    ]
+    indices = [
+        remote(ref_hbm, ref_next, index_send.at[0], index_recv.at[0], (prev, az, rg)),
+        remote(sec_hbm, sec_next, index_send.at[1], index_recv.at[1], (prev, az, rg)),
+        remote(ref_hbm, ref_prev, index_send.at[2], index_recv.at[2], (nxt, az, rg)),
+        remote(sec_hbm, sec_prev, index_send.at[3], index_recv.at[3], (nxt, az, rg)),
+    ]
+    for copy in indices[2:]:
+        copy.start()
+    for copy in tiles:
+        copy.start()
+    for a in (2, 1, 0):
+        slabs[a].start()
 
     col = lax.broadcasted_iota(jnp.int32, (128, 128), 1) * 20
     row = lax.broadcasted_iota(jnp.int32, (128, 128), 0)
@@ -73,39 +105,6 @@
             sample = sample - (128 * WIDE) * rg
         inside = (sample >= col - 10) & (sample <= col + 30)
         table[pl.ds(128 * t, 128), :] = jnp.where(inside, 1.0, 0.0).astype(BF16)
-
-    pl.semaphore_wait(barrier, len(peers))
-
-    def remote(src, dst, send, recv, device):
-        return pltpu.make_async_remote_copy(
-            src_ref=src, dst_ref=dst, send_sem=send, recv_sem=recv,
-            device_id=device, device_id_type=MESH,
-        )
-
-    slabs = [
-        remote(acq.at[ACQ - EDGE + a], edge.at[a, :, pl.ds(0, TILES)],
-               slab_send.at[a], slab_recv.at[a], (nxt, az, rg))
-        for a in range(EDGE)
-    ]
-    border = (TILES - 1) * org
-    tiles = [
-        remote(acq.at[:, :, border], block.at[:, :, TILES],
-               tile_send.at[0], tile_recv.at[0], (d, az, org)),
-        remote(acq.at[pl.ds(ACQ - EDGE, EDGE), :, border], edge.at[:, :, TILES],
-               tile_send.at[1], tile_recv.at[1], (nxt, az, org)),
-    ]
-    indices = [
-        remote(ref_hbm, ref_next, index_send.at[0], index_recv.at[0], (prev, az, rg)),
-        remote(sec_hbm, sec_next, index_send.at[1], index_recv.at[1], (prev, az, rg)),
-        remote(ref_hbm, ref_prev, index_send.at[2], index_recv.at[2], (nxt, az, rg)),
-        remote(sec_hbm, sec_prev, index_send.at[3], index_recv.at[3], (nxt, az, rg)),
-    ]
-    for copy in indices:
-        copy.start()
-    for copy in tiles:
-        copy.start()
-    for a in (2, 1, 0):
-        slabs[a].start()
 
     def line(ref, a, l):
         start = a * ROWS + l * (2 * WIDE)
@@ -192,18 +191,30 @@
 
     for copy in own[1:]:
         copy.wait()
-    for copy in indices:
-        copy.wait_recv()
     names = [(ref_prev, sec_prev), (ref_own, sec_own), (ref_next, sec_next)]
 
     def clip(i):
         return jnp.clip(i, 0, ACQ - 1)
 
-    for g, (refs, secs) in enumerate(names):
-        def cross_step(k, carry, g=g, refs=refs, secs=secs):
+    def group(g):
+        refs, secs = names[g]
+
+        def cross_step(k, carry):
             cross(2 * (SLOTS * g + k), wide, clip(refs[k] - base), clip(secs[k] - base))
             return carry
+
         lax.fori_loop(0, SLOTS, cross_step, 0)
+
+    group(1)
+    pl.semaphore_wait(ready, 2)
+    for copy in indices[:2]:
+        copy.start()
+    for copy in indices[2:]:
+        copy.wait_recv()
+    group(0)
+    for copy in indices[:2]:
+        copy.wait_recv()
+    group(2)
 
     range_sums(0, EARLY, early)
 
@@ -272,7 +283,6 @@
     window = lax.broadcasted_iota(jnp.int32, (4, 128), 0)
     shared = window == 3 * oaz
     for k in range(SLOTS):
-        live = k < count[0]
         for c in range(4):
             i = 4 * k + c
             rim = in_b[0, pl.ds(i, 1), :] + in_b[1, pl.ds(i, 1), :] + in_b[2, pl.ds(i, 1), :]
@@ -281,30 +291,30 @@
                 j = 2 * k + c
                 rim = rim + in_late_b[0, pl.ds(j, 1), :] + in_late_b[1, pl.ds(j, 1), :]
                 body = body + late_a[1, j] + in_late_a[j]
-            total = body + jnp.where(shared, rim, 0.0)
-            if c < 2:
-                total = jnp.where(live, total, jnp.zeros((4, 128), F32))
-            totals[k, c] = total
-
-
-def finish(totals, ifg, coh):
+            totals[k, c] = body + jnp.where(shared, rim, 0.0)
+
+
+def finish(totals, count, ifg, coh):
+    slot = lax.broadcasted_iota(jnp.int32, (SLOTS, 4, 128), 0)
+    live = slot < count[...].reshape(1, 1, 1)
     re, im = totals[:, 0], totals[:, 1]
-    ifg[:, 0] = re / 451.0
-    ifg[:, 1] = im / 451.0
-    coh[...] = jnp.sqrt(re * re + im * im) / jnp.sqrt(totals[:, 2] * totals[:, 3] + 1e-06)
+    value = jnp.sqrt(re * re + im * im) / jnp.sqrt(totals[:, 2] * totals[:, 3] + 1e-06)
+    ifg[:, 0] = jnp.where(live, re / 451.0, 0.0)
+    ifg[:, 1] = jnp.where(live, im / 451.0, 0.0)
+    coh[...] = jnp.where(live, value, 0.0)
 
 
 def on_device(acquisitions, reference_index, secondary_index, pair_count):
     view = acquisitions.reshape(ACQ, 2, LINES, TILES, 128)
     view = with_layout_constraint(view, Layout((0, 2, 3, 1, 4)))
     view = view.transpose(0, 2, 3, 1, 4)
-    hbm = pl.BlockSpec(memory_space=pl.ANY)
+    hbm = pl.BlockSpec(memory_space=pltpu.HBM)
     vmem = pl.BlockSpec(memory_space=pltpu.VMEM)
     dma = pltpu.SemaphoreType.DMA
     totals = pl.pallas_call(
         kernel,
-        out_shape=jax.ShapeDtypeStruct((SLOTS, 4, 4, 128), F32),
-        in_specs=[hbm] * 4,
+        out_shape=pltpu.VMEM((SLOTS, 4, 4, 128), F32),
+        in_specs=[hbm] * 3,
         out_specs=vmem,
         scratch_shapes=[
             pltpu.VMEM((ACQ, LINES, WIDE, 2, 128), BF16),
@@ -324,23 +334,25 @@
             pltpu.VMEM((2, 8, 128), F32),
             pltpu.VMEM((8, 4, 128), F32),
             pltpu.VMEM((2, 8, 128), F32),
-        ] + [pltpu.SMEM((SLOTS,), jnp.int32)] * 6 + [pltpu.SMEM((1,), jnp.int32)] + [
-            dma((4,)), dma((EDGE,)), dma((EDGE,)), dma((2,)), dma((2,)),
+        ] + [pltpu.SMEM((SLOTS,), jnp.int32)] * 6 + [
+            dma((3,)), dma((EDGE,)), dma((EDGE,)), dma((2,)), dma((2,)),
             dma((4,)), dma((4,)), dma((5,)), dma((5,)), dma((3,)), dma((3,)),
+            pltpu.SemaphoreType.REGULAR,
         ],
         compiler_params=pltpu.CompilerParams(
             collective_id=0, has_side_effects=True, vmem_limit_bytes=60 * 2**20
         ),
-    )(view, reference_index, secondary_index, pair_count)
+    )(view, reference_index, secondary_index)
     return pl.pallas_call(
         finish,
         out_shape=(
             jax.ShapeDtypeStruct((SLOTS, 2, 4, 128), F32),
             jax.ShapeDtypeStruct((SLOTS, 4, 128), F32),
         ),
-        in_specs=[vmem],
+        in_specs=[vmem, vmem],
         out_specs=(vmem, vmem),
-    )(totals)
+        compiler_params=pltpu.CompilerParams(vmem_limit_bytes=2**20),
+    )(totals, pair_count.reshape(1, 1))
 
 
 def solution(mesh):

time: 36.5 us -> 32.4 us (0.89)
  the two profiles are of different devices: /device:TPU:1 before, /device:TPU:2 now
where the time goes in v3:
time: 32.4 us; the launch traced here: 32.3 us
  Pallas kernels  31 us (96%)
  between operations  1.29 us (4%)
    pallas_call x1, Pallas kernels, on_device(): pl.pallas_call(kernel, out_shape=pltpu.VMEM((SLOTS, 4, 4, 128), F32), in_...  30.3 us
    pallas_call x1, Pallas kernels, on_device(): pl.pallas_call(finish, out_shape=(jax.ShapeDtypeStruct((SLOTS, 2, 4, 128)...  0.68 us

profile of v3, /device:TPU:2, one launch (start us, length us, event | category | flops | bytes accessed | tf_op | source)
XLA Modules:
  0.0 32.3 jit_solution(14365715757802952033)
XLA Ops:
  1.3 30.3 %shard_map.59.totals = f32[4,4,4,128]{3,2,1,0:T(4,128)S(1)} custom-call(bf16[16,20,20,2,128]{4,3,2,1,0:T(2,128)(2,1)} %bitcast.5, s32[4]{0:T(128)} %ref_hbm.1, s32[4]{0:T(128)} %sec_hbm.1), custom_call_target="tpu_custom_call" | custom-call | tf_op jit(solution)/shard_map/pallas_call | solution.py:314
  31.6 0.7 %shard_map.60 = (f32[4,2,4,128]{3,2,1,0:T(4,128)}, f32[4,4,128]{2,1,0:T(4,128)}) custom-call(f32[4,4,4,128]{3,2,1,0:T(4,128)S(1)} %shard_map.59.totals, s32[1,1]{1,0:T(1,128)} %bitcast.4.count), custom_call_target="tpu_custom_call" | custom-call | tf_op jit(solution)/shard_map/pallas_call | solution.py:346

commit v4 on v3

--- a/solution.py
+++ b/solution.py
@@ -12,8 +12,10 @@
 LINES = 20
 TILES = 20
 WIDE = TILES + 1
+COMBOS = ((1, 0), (1, 1), (1, 2), (2, 0), (2, 1), (3, 0))
+FORWARD = 5
+TURN = 16
 EDGE = 3
-COMBOS = ((2, 0), (2, 1), (2, 2), (1, 0), (1, 1), (0, 0))
 CROSS = 2 * 3 * SLOTS
 EARLY = CROSS + ACQ
 LATE = 2 * len(COMBOS)
@@ -63,7 +65,7 @@
         pl.semaphore_signal(barrier, inc=1, device_id=peer, device_id_type=MESH)
 
     pl.semaphore_wait(barrier, len(peers))
-    for peer in ((nxt, az, rg), (nxt, oaz, rg)):
+    for peer in ((nxt, az, rg), (nxt, oaz, rg), (nxt, az, org)):
         pl.semaphore_signal(ready, inc=1, device_id=peer, device_id_type=MESH)
 
     def remote(src, dst, send, recv, device):
@@ -73,16 +75,21 @@
         )
 
     slabs = [
-        remote(acq.at[ACQ - EDGE + a], edge.at[a, :, pl.ds(0, TILES)],
-               slab_send.at[a], slab_recv.at[a], (nxt, az, rg))
-        for a in range(EDGE)
+        remote(acq.at[ACQ - 2], edge.at[0, :, pl.ds(0, TILES)],
+               slab_send.at[0], slab_recv.at[0], (nxt, az, rg)),
+        remote(acq.at[ACQ - 1], edge.at[1, :, pl.ds(0, TILES)],
+               slab_send.at[1], slab_recv.at[1], (nxt, az, rg)),
+        remote(acq.at[0], edge.at[2, :, pl.ds(0, TILES)],
+               slab_send.at[2], slab_recv.at[2], (prev, az, rg)),
     ]
     border = (TILES - 1) * org
     tiles = [
         remote(acq.at[:, :, border], block.at[:, :, TILES],
                tile_send.at[0], tile_recv.at[0], (d, az, org)),
-        remote(acq.at[pl.ds(ACQ - EDGE, EDGE), :, border], edge.at[:, :, TILES],
+        remote(acq.at[pl.ds(ACQ - 2, 2), :, border], edge.at[pl.ds(0, 2), :, TILES],
                tile_send.at[1], tile_recv.at[1], (nxt, az, org)),
+        remote(acq.at[0, :, border], edge.at[2, :, TILES],
+               tile_send.at[2], tile_recv.at[2], (prev, az, org)),
     ]
     indices = [
         remote(ref_hbm, ref_next, index_send.at[0], index_recv.at[0], (prev, az, rg)),
@@ -92,9 +99,9 @@
     ]
     for copy in indices[2:]:
         copy.start()
-    for copy in tiles:
+    for copy in tiles[:2]:
         copy.start()
-    for a in (2, 1, 0):
+    for a in (1, 0):
         slabs[a].start()
 
     col = lax.broadcasted_iota(jnp.int32, (128, 128), 1) * 20
@@ -154,10 +161,10 @@
             return (x * x + y * y,)
         line_sums(plane, get)
 
-    def cross(plane, one, a, b):
+    def cross(plane, one, a, two, b):
         def get(l):
             xr, yr = line(one, a, l)
-            xs, ys = line(wide, b, l)
+            xs, ys = line(two, b, l)
             return (xr * xs + yr * ys, yr * xs - xr * ys)
         line_sums(plane, get)
 
@@ -200,15 +207,17 @@
         refs, secs = names[g]
 
         def cross_step(k, carry):
-            cross(2 * (SLOTS * g + k), wide, clip(refs[k] - base), clip(secs[k] - base))
+            cross(2 * (SLOTS * g + k), wide, clip(refs[k] - base), wide, clip(secs[k] - base))
             return carry
 
         lax.fori_loop(0, SLOTS, cross_step, 0)
 
     group(1)
-    pl.semaphore_wait(ready, 2)
+    pl.semaphore_wait(ready, 3)
     for copy in indices[:2]:
         copy.start()
+    tiles[2].start()
+    slabs[2].start()
     for copy in indices[2:]:
         copy.wait_recv()
     group(0)
@@ -219,15 +228,21 @@
     range_sums(0, EARLY, early)
 
     zero = jnp.zeros((8, 128), F32)
-    for g, (refs, secs) in enumerate(names):
+
+    def collect(g, behind):
+        refs, secs = names[g]
         for k in range(SLOTS):
             r = refs[k] - base
             s = secs[k] - base
             has_r = (r >= 0) & (r < ACQ)
             has_s = (s >= 0) & (s < ACQ)
+            reach = ((r == -1) | (r == -2)) & has_s
+            combo = jnp.clip(jnp.where(r == -1, s, s + 3), 0, FORWARD - 1)
             for c in range(4):
                 if c < 2:
                     value = jnp.where(has_r & has_s, early[2 * (SLOTS * g + k) + c], zero)
+                    if behind:
+                        value = value + jnp.where(reach, late[2 * combo + c], zero)
                 elif c == 2:
                     value = jnp.where(has_r, early[CROSS + clip(r)], zero)
                 else:
@@ -235,46 +250,67 @@
                 out_a[g, 4 * k + c] = value[0:4]
                 out_b[g, pl.ds(4 * k + c, 1), :] = value[4:5]
 
+    collect(2, False)
     backs = [
-        remote(out_a.at[2], in_a.at[0], back_send.at[1], back_recv.at[1], (nxt, az, rg)),
-        remote(out_b.at[2], in_b.at[0], back_send.at[4], back_recv.at[4], (nxt, oaz, rg)),
-        remote(out_a.at[0], in_a.at[1], back_send.at[0], back_recv.at[0], (prev, az, rg)),
-        remote(out_b.at[0], in_b.at[2], back_send.at[2], back_recv.at[2], (prev, oaz, rg)),
-        remote(out_b.at[1], in_b.at[1], back_send.at[3], back_recv.at[3], (d, oaz, rg)),
-    ]
-    for copy in backs:
+        remote(out_a.at[2], in_a.at[0], back_send.at[0], back_recv.at[0], (nxt, az, rg)),
+        remote(out_b.at[2], in_b.at[0], back_send.at[1], back_recv.at[1], (nxt, oaz, rg)),
+        remote(out_a.at[0], in_a.at[1], back_send.at[2], back_recv.at[2], (prev, az, rg)),
+        remote(out_b.at[0], in_b.at[2], back_send.at[3], back_recv.at[3], (prev, oaz, rg)),
+        remote(out_b.at[1], in_b.at[1], back_send.at[4], back_recv.at[4], (d, oaz, rg)),
+    ]
+    for copy in backs[:2]:
         copy.start()
 
-    tiles[1].wait_recv()
-    for a in (2, 1, 0):
+    def widen_edge(a):
         slabs[a].wait_recv()
         wide_edge[pl.ds(a * ROWS, ROWS), :] = edge[a].reshape(ROWS, 128).astype(F32)
-        for i, (r, s) in enumerate(COMBOS):
-            if r == a:
-                cross(2 * i, wide_edge, r, s)
-        if a == 1:
-            range_sums(0, 10, late)
-    range_sums(10, 2, late)
-
-    for g, (refs, secs) in enumerate(names[:2]):
-        for k in range(SLOTS):
-            r = refs[k] - base
-            s = secs[k] - base
-            reach = (r < 0) & (s >= 0) & (s < ACQ)
-            combo = jnp.where(r == -1, s, jnp.where(r == -2, s + 3, 5))
-            combo = jnp.clip(combo, 0, len(COMBOS) - 1)
-            for c in range(2):
-                value = jnp.where(reach, late[2 * combo + c], zero)
-                late_a[g, 2 * k + c] = value[0:4]
-                late_b[g, pl.ds(2 * k + c, 1), :] = value[4:5]
 
     lates = [
-        remote(late_a.at[0], in_late_a, late_send.at[0], late_recv.at[0], (prev, az, rg)),
-        remote(late_b.at[0], in_late_b.at[0], late_send.at[1], late_recv.at[1], (prev, oaz, rg)),
-        remote(late_b.at[1], in_late_b.at[1], late_send.at[2], late_recv.at[2], (d, oaz, rg)),
-    ]
-    for copy in lates:
-        copy.start()
+        remote(late_a.at[1], in_late_a, late_send.at[0], late_recv.at[0], (nxt, az, rg)),
+        remote(late_b.at[1], in_late_b, late_send.at[1], late_recv.at[1], (nxt, oaz, rg)),
+    ]
+
+    def reach_back():
+        tiles[1].wait_recv()
+        for a, far in ((1, 1), (0, 2)):
+            widen_edge(a)
+            for i, (r, s) in enumerate(COMBOS[:FORWARD]):
+                if r == far:
+                    cross(2 * i, wide_edge, a, wide, s)
+        range_sums(0, 2 * FORWARD, late)
+        collect(0, True)
+        for copy in backs[2:4]:
+            copy.start()
+        collect(1, True)
+
+    def reach_ahead():
+        tiles[2].wait_recv()
+        widen_edge(2)
+        cross(2 * FORWARD, wide, ACQ - 3, wide_edge, 2)
+        range_sums(2 * FORWARD, 2, late)
+        for g in (2, 1):
+            refs, secs = names[g]
+            for k in range(SLOTS):
+                reach = (refs[k] - base == ACQ - 3) & (secs[k] - base == ACQ)
+                for c in range(2):
+                    value = jnp.where(reach, late[2 * FORWARD + c], zero)
+                    late_a[g - 1, 2 * k + c] = value[0:4]
+                    late_b[g - 1, pl.ds(2 * k + c, 1), :] = value[4:5]
+            if g == 2:
+                for copy in lates:
+                    copy.start()
+
+    turned = lax.rem(d, TURN) == TURN - 1
+    pl.when(turned)(reach_ahead)
+    reach_back()
+    pl.when(jnp.logical_not(turned))(reach_ahead)
+
+    for k in range(SLOTS):
+        for c in range(2):
+            i, j = 4 * k + c, 2 * k + c
+            out_a[1, i] = out_a[1, i] + late_a[0, j]
+            out_b[1, pl.ds(i, 1), :] = out_b[1, pl.ds(i, 1), :] + late_b[0, pl.ds(j, 1), :]
+    backs[4].start()
     for copy in tiles + indices + slabs:
         copy.wait_send()
     for copy in backs + lates:
@@ -289,8 +325,8 @@
             body = out_a[1, i] + in_a[0, i] + in_a[1, i]
             if c < 2:
                 j = 2 * k + c
-                rim = rim + in_late_b[0, pl.ds(j, 1), :] + in_late_b[1, pl.ds(j, 1), :]
-                body = body + late_a[1, j] + in_late_a[j]
+                rim = rim + in_late_b[pl.ds(j, 1), :]
+                body = body + in_late_a[j]
             totals[k, c] = body + jnp.where(shared, rim, 0.0)
 
 
@@ -333,10 +369,10 @@
             pltpu.VMEM((2, 8, 4, 128), F32),
             pltpu.VMEM((2, 8, 128), F32),
             pltpu.VMEM((8, 4, 128), F32),
-            pltpu.VMEM((2, 8, 128), F32),
+            pltpu.VMEM((8, 128), F32),
         ] + [pltpu.SMEM((SLOTS,), jnp.int32)] * 6 + [
-            dma((3,)), dma((EDGE,)), dma((EDGE,)), dma((2,)), dma((2,)),
-            dma((4,)), dma((4,)), dma((5,)), dma((5,)), dma((3,)), dma((3,)),
+            dma((3,)), dma((EDGE,)), dma((EDGE,)), dma((3,)), dma((3,)),
+            dma((4,)), dma((4,)), dma((5,)), dma((5,)), dma((2,)), dma((2,)),
             pltpu.SemaphoreType.REGULAR,
         ],
         compiler_params=pltpu.CompilerParams(

time: 32.4 us -> 31.1 us (0.960)
  the two profiles are of different devices: /device:TPU:2 before, /device:TPU:1 now
where the time goes in v4:
time: 31.1 us; the launch traced here: 31 us
  Pallas kernels  29.7 us (95%)
  between operations  1.29 us (4%)
    pallas_call x1, Pallas kernels, on_device(): pl.pallas_call(kernel, out_shape=pltpu.VMEM((SLOTS, 4, 4, 128), F32), in_...  29 us
    pallas_call x1, Pallas kernels, on_device(): pl.pallas_call(finish, out_shape=(jax.ShapeDtypeStruct((SLOTS, 2, 4, 128)...  0.68 us

profile of v4, /device:TPU:1, one launch (start us, length us, event | category | flops | bytes accessed | tf_op | source)
XLA Modules:
  0.0 31.0 jit_solution(16996875987096992803)
XLA Ops:
  1.3 29.0 %shard_map.59.totals = f32[4,4,4,128]{3,2,1,0:T(4,128)S(1)} custom-call(bf16[16,20,20,2,128]{4,3,2,1,0:T(2,128)(2,1)} %bitcast.5, s32[4]{0:T(128)} %ref_hbm.1, s32[4]{0:T(128)} %sec_hbm.1), custom_call_target="tpu_custom_call" | custom-call | tf_op jit(solution)/shard_map/pallas_call | solution.py:350
  30.3 0.7 %shard_map.60 = (f32[4,2,4,128]{3,2,1,0:T(4,128)}, f32[4,4,128]{2,1,0:T(4,128)}) custom-call(f32[4,4,4,128]{3,2,1,0:T(4,128)S(1)} %shard_map.59.totals, s32[1,1]{1,0:T(1,128)} %bitcast.4.count), custom_call_target="tpu_custom_call" | custom-call | tf_op jit(solution)/shard_map/pallas_call | solution.py:382

commit v5 on v4

--- a/solution.py
+++ b/solution.py
@@ -180,6 +180,16 @@
         total = both[:rows] + both[rows:]
         result[pl.ds(first, planes)] = total.reshape(planes, 8, 128)
 
+    def send_back():
+        pl.semaphore_wait(ready, 3)
+        for copy in indices[:2]:
+            copy.start()
+        tiles[2].start()
+        slabs[2].start()
+
+    soon = lax.rem(d, 2) == 1
+    pl.when(soon)(send_back)
+
     own[0].wait()
     tiles[0].wait_recv()
 
@@ -213,11 +223,7 @@
         lax.fori_loop(0, SLOTS, cross_step, 0)
 
     group(1)
-    pl.semaphore_wait(ready, 3)
-    for copy in indices[:2]:
-        copy.start()
-    tiles[2].start()
-    slabs[2].start()
+    pl.when(jnp.logical_not(soon))(send_back)
     for copy in indices[2:]:
         copy.wait_recv()
     group(0)

time: 31.1 us -> 30 us (0.965)
  Pallas kernels: 29.7 us -> 28.6 us
    pallas_call x1, Pallas kernels: 29 us -> 27.9 us  [on_device(): pl.pallas_call(kernel, out_shape=pltpu.VMEM((SLOTS, 4, 4, 128), F32), in_...]
where the time goes in v5:
time: 30 us; the launch traced here: 29.9 us
  Pallas kernels  28.6 us (95%)
  between operations  1.29 us (4%)
    pallas_call x1, Pallas kernels, on_device(): pl.pallas_call(kernel, out_shape=pltpu.VMEM((SLOTS, 4, 4, 128), F32), in_...  27.9 us
    pallas_call x1, Pallas kernels, on_device(): pl.pallas_call(finish, out_shape=(jax.ShapeDtypeStruct((SLOTS, 2, 4, 128)...  0.68 us

profile of v5, /device:TPU:1, one launch (start us, length us, event | category | flops | bytes accessed | tf_op | source)
XLA Modules:
  0.0 29.9 jit_solution(1957216653624399680)
XLA Ops:
  1.3 27.9 %shard_map.59.totals = f32[4,4,4,128]{3,2,1,0:T(4,128)S(1)} custom-call(bf16[16,20,20,2,128]{4,3,2,1,0:T(2,128)(2,1)} %bitcast.5, s32[4]{0:T(128)} %ref_hbm.1, s32[4]{0:T(128)} %sec_hbm.1), custom_call_target="tpu_custom_call" | custom-call | tf_op jit(solution)/shard_map/pallas_call | solution.py:356
  29.2 0.7 %shard_map.60 = (f32[4,2,4,128]{3,2,1,0:T(4,128)}, f32[4,4,128]{2,1,0:T(4,128)}) custom-call(f32[4,4,4,128]{3,2,1,0:T(4,128)S(1)} %shard_map.59.totals, s32[1,1]{1,0:T(1,128)} %bitcast.4.count), custom_call_target="tpu_custom_call" | custom-call | tf_op jit(solution)/shard_map/pallas_call | solution.py:388

commit v6 on v5

--- a/solution.py
+++ b/solution.py
@@ -1,3 +1,5 @@
+import functools
+
 import jax
 import jax.numpy as jnp
 from jax import lax
@@ -46,6 +48,7 @@
 
     prev, nxt = at(-1), at(1)
     base = ACQ * d
+    has_prev, has_next = d > 0, d < n - 1
     upper = az == 0
 
     own = [
@@ -57,16 +60,21 @@
         copy.start()
 
     barrier = pltpu.get_barrier_semaphore()
-    peers = [
-        (d, az, org), (d, oaz, rg),
-        (prev, az, rg), (prev, az, org), (prev, oaz, rg),
-    ]
-    for peer in peers:
-        pl.semaphore_signal(barrier, inc=1, device_id=peer, device_id_type=MESH)
-
-    pl.semaphore_wait(barrier, len(peers))
-    for peer in ((nxt, az, rg), (nxt, oaz, rg), (nxt, az, org)):
-        pl.semaphore_signal(ready, inc=1, device_id=peer, device_id_type=MESH)
+    def greet(semaphore, peers):
+        for peer in peers:
+            pl.semaphore_signal(semaphore, inc=1, device_id=peer, device_id_type=MESH)
+
+    greet(barrier, [(d, az, org), (d, oaz, rg)])
+
+    @pl.when(has_prev)
+    def _():
+        greet(barrier, [(prev, az, rg), (prev, az, org), (prev, oaz, rg)])
+
+    pl.semaphore_wait(barrier, jnp.where(has_next, 5, 2))
+
+    @pl.when(has_next)
+    def _():
+        greet(ready, [(nxt, az, rg), (nxt, oaz, rg), (nxt, az, org)])
 
     def remote(src, dst, send, recv, device):
         return pltpu.make_async_remote_copy(
@@ -74,28 +82,67 @@
             device_id=device, device_id_type=MESH,
         )
 
+    class Toward:
+        def __init__(self, step, *parts):
+            self.copy = remote(*parts)
+            self.sends, self.receives = (
+                (has_next, has_prev) if step > 0 else (has_prev, has_next)
+            )
+
+        def start(self):
+            pl.when(self.sends)(self.copy.start)
+
+        def wait_send(self):
+            pl.when(self.sends)(self.copy.wait_send)
+
+        def wait_recv(self):
+            pl.when(self.receives)(self.copy.wait_recv)
+
+        def wait(self):
+            self.wait_send()
+            self.wait_recv()
+
+    forward = functools.partial(Toward, 1)
+    backward = functools.partial(Toward, -1)
+
+    @pl.when(jnp.logical_not(has_prev))
+    def _():
+        for ref in (in_a.at[0], in_b.at[0], in_late_a, in_late_b):
+            ref[...] = jnp.zeros(ref.shape, F32)
+        for k in range(SLOTS):
+            ref_prev[k] = 0
+            sec_prev[k] = 0
+
+    @pl.when(jnp.logical_not(has_next))
+    def _():
+        for ref in (in_a.at[1], in_b.at[2]):
+            ref[...] = jnp.zeros(ref.shape, F32)
+        for k in range(SLOTS):
+            ref_next[k] = 0
+            sec_next[k] = 0
+
     slabs = [
-        remote(acq.at[ACQ - 2], edge.at[0, :, pl.ds(0, TILES)],
+        forward(acq.at[ACQ - 2], edge.at[0, :, pl.ds(0, TILES)],
                slab_send.at[0], slab_recv.at[0], (nxt, az, rg)),
-        remote(acq.at[ACQ - 1], edge.at[1, :, pl.ds(0, TILES)],
+        forward(acq.at[ACQ - 1], edge.at[1, :, pl.ds(0, TILES)],
                slab_send.at[1], slab_recv.at[1], (nxt, az, rg)),
-        remote(acq.at[0], edge.at[2, :, pl.ds(0, TILES)],
+        backward(acq.at[0], edge.at[2, :, pl.ds(0, TILES)],
                slab_send.at[2], slab_recv.at[2], (prev, az, rg)),
     ]
     border = (TILES - 1) * org
     tiles = [
         remote(acq.at[:, :, border], block.at[:, :, TILES],
                tile_send.at[0], tile_recv.at[0], (d, az, org)),
-        remote(acq.at[pl.ds(ACQ - 2, 2), :, border], edge.at[pl.ds(0, 2), :, TILES],
+        forward(acq.at[pl.ds(ACQ - 2, 2), :, border], edge.at[pl.ds(0, 2), :, TILES],
                tile_send.at[1], tile_recv.at[1], (nxt, az, org)),
-        remote(acq.at[0, :, border], edge.at[2, :, TILES],
+        backward(acq.at[0, :, border], edge.at[2, :, TILES],
                tile_send.at[2], tile_recv.at[2], (prev, az, org)),
     ]
     indices = [
-        remote(ref_hbm, ref_next, index_send.at[0], index_recv.at[0], (prev, az, rg)),
-        remote(sec_hbm, sec_next, index_send.at[1], index_recv.at[1], (prev, az, rg)),
-        remote(ref_hbm, ref_prev, index_send.at[2], index_recv.at[2], (nxt, az, rg)),
-        remote(sec_hbm, sec_prev, index_send.at[3], index_recv.at[3], (nxt, az, rg)),
+        backward(ref_hbm, ref_next, index_send.at[0], index_recv.at[0], (prev, az, rg)),
+        backward(sec_hbm, sec_next, index_send.at[1], index_recv.at[1], (prev, az, rg)),
+        forward(ref_hbm, ref_prev, index_send.at[2], index_recv.at[2], (nxt, az, rg)),
+        forward(sec_hbm, sec_prev, index_send.at[3], index_recv.at[3], (nxt, az, rg)),
     ]
     for copy in indices[2:]:
         copy.start()
@@ -181,7 +228,7 @@
         result[pl.ds(first, planes)] = total.reshape(planes, 8, 128)
 
     def send_back():
-        pl.semaphore_wait(ready, 3)
+        pl.when(has_prev)(lambda: pl.semaphore_wait(ready, 3))
         for copy in indices[:2]:
             copy.start()
         tiles[2].start()
@@ -258,10 +305,10 @@
 
     collect(2, False)
     backs = [
-        remote(out_a.at[2], in_a.at[0], back_send.at[0], back_recv.at[0], (nxt, az, rg)),
-        remote(out_b.at[2], in_b.at[0], back_send.at[1], back_recv.at[1], (nxt, oaz, rg)),
-        remote(out_a.at[0], in_a.at[1], back_send.at[2], back_recv.at[2], (prev, az, rg)),
-        remote(out_b.at[0], in_b.at[2], back_send.at[3], back_recv.at[3], (prev, oaz, rg)),
+        forward(out_a.at[2], in_a.at[0], back_send.at[0], back_recv.at[0], (nxt, az, rg)),
+        forward(out_b.at[2], in_b.at[0], back_send.at[1], back_recv.at[1], (nxt, oaz, rg)),
+        backward(out_a.at[0], in_a.at[1], back_send.at[2], back_recv.at[2], (prev, az, rg)),
+        backward(out_b.at[0], in_b.at[2], back_send.at[3], back_recv.at[3], (prev, oaz, rg)),
         remote(out_b.at[1], in_b.at[1], back_send.at[4], back_recv.at[4], (d, oaz, rg)),
     ]
     for copy in backs[:2]:
@@ -272,8 +319,8 @@
         wide_edge[pl.ds(a * ROWS, ROWS), :] = edge[a].reshape(ROWS, 128).astype(F32)
 
     lates = [
-        remote(late_a.at[1], in_late_a, late_send.at[0], late_recv.at[0], (nxt, az, rg)),
-        remote(late_b.at[1], in_late_b, late_send.at[1], late_recv.at[1], (nxt, oaz, rg)),
+        forward(late_a.at[1], in_late_a, late_send.at[0], late_recv.at[0], (nxt, az, rg)),
+        forward(late_b.at[1], in_late_b, late_send.at[1], late_recv.at[1], (nxt, oaz, rg)),
     ]
 
     def reach_back():

time: 30 us -> 29.1 us (0.970)
  the two profiles are of different devices: /device:TPU:1 before, /device:TPU:232 now
where the time goes in v6:
time: 29.1 us; the launch traced here: 29 us
  Pallas kernels  27.7 us (95%)
  between operations  1.29 us (4%)
    pallas_call x1, Pallas kernels, on_device(): pl.pallas_call(kernel, out_shape=pltpu.VMEM((SLOTS, 4, 4, 128), F32), in_...  27 us
    pallas_call x1, Pallas kernels, on_device(): pl.pallas_call(finish, out_shape=(jax.ShapeDtypeStruct((SLOTS, 2, 4, 128)...  0.68 us

profile of v6, /device:TPU:232, one launch (start us, length us, event | category | flops | bytes accessed | tf_op | source)
XLA Modules:
  0.0 29.0 jit_solution(10715475794025326195)
XLA Ops:
  1.3 27.0 %shard_map.59.totals = f32[4,4,4,128]{3,2,1,0:T(4,128)S(1)} custom-call(bf16[16,20,20,2,128]{4,3,2,1,0:T(2,128)(2,1)} %bitcast.5, s32[4]{0:T(128)} %ref_hbm.1, s32[4]{0:T(128)} %sec_hbm.1), custom_call_target="tpu_custom_call" | custom-call | tf_op jit(solution)/shard_map/pallas_call | solution.py:403
  28.3 0.7 %shard_map.60 = (f32[4,2,4,128]{3,2,1,0:T(4,128)}, f32[4,4,128]{2,1,0:T(4,128)}) custom-call(f32[4,4,4,128]{3,2,1,0:T(4,128)S(1)} %shard_map.59.totals, s32[1,1]{1,0:T(1,128)} %bitcast.4.count), custom_call_target="tpu_custom_call" | custom-call | tf_op jit(solution)/shard_map/pallas_call | solution.py:435

commit v7 on v6

--- a/solution.py
+++ b/solution.py
@@ -146,10 +146,10 @@
     ]
     for copy in indices[2:]:
         copy.start()
-    for copy in tiles[:2]:
-        copy.start()
+    tiles[0].start()
     for a in (1, 0):
         slabs[a].start()
+    tiles[1].start()
 
     col = lax.broadcasted_iota(jnp.int32, (128, 128), 1) * 20
     row = lax.broadcasted_iota(jnp.int32, (128, 128), 0)
@@ -231,8 +231,8 @@
         pl.when(has_prev)(lambda: pl.semaphore_wait(ready, 3))
         for copy in indices[:2]:
             copy.start()
+        slabs[2].start()
         tiles[2].start()
-        slabs[2].start()
 
     soon = lax.rem(d, 2) == 1
     pl.when(soon)(send_back)

time: 29.1 us -> 28.9 us (level)
  the two profiles are of different devices: /device:TPU:232 before, /device:TPU:1 now
where the time goes in v7:
time: 28.9 us; the launch traced here: 28.5 us
  Pallas kernels  27.2 us (94%)
  between operations  1.29 us (4%)
    pallas_call x1, Pallas kernels, on_device(): pl.pallas_call(kernel, out_shape=pltpu.VMEM((SLOTS, 4, 4, 128), F32), in_...  26.5 us
    pallas_call x1, Pallas kernels, on_device(): pl.pallas_call(finish, out_shape=(jax.ShapeDtypeStruct((SLOTS, 2, 4, 128)...  0.68 us

profile of v7, /device:TPU:1, one launch (start us, length us, event | category | flops | bytes accessed | tf_op | source)
XLA Modules:
  0.0 28.5 jit_solution(10527747172552017170)
XLA Ops:
  1.3 26.5 %shard_map.59.totals = f32[4,4,4,128]{3,2,1,0:T(4,128)S(1)} custom-call(bf16[16,20,20,2,128]{4,3,2,1,0:T(2,128)(2,1)} %bitcast.5, s32[4]{0:T(128)} %ref_hbm.1, s32[4]{0:T(128)} %sec_hbm.1), custom_call_target="tpu_custom_call" | custom-call | tf_op jit(solution)/shard_map/pallas_call | solution.py:403
  27.8 0.7 %shard_map.60 = (f32[4,2,4,128]{3,2,1,0:T(4,128)}, f32[4,4,128]{2,1,0:T(4,128)}) custom-call(f32[4,4,4,128]{3,2,1,0:T(4,128)S(1)} %shard_map.59.totals, s32[1,1]{1,0:T(1,128)} %bitcast.4.count), custom_call_target="tpu_custom_call" | custom-call | tf_op jit(solution)/shard_map/pallas_call | solution.py:435
